TPU v7x, 256 devices: a whole 4x4x8 slice. The times are simulated.
256 devices in a mesh: grp: 2 (over core), seq: 32 (over y, z), tp: 4 (over x).
Axes of the slice: x: 4, y: 4, z: 8, core: 2. Of those that a mesh axis runs over, the one named last changes fastest.
Arguments:
- patches_in: bfloat16 [65536, 1280], P(('grp', 'seq')), may hold values from -6 to 6
- gain_attn: float32 [1280], replicated, may hold values from 0.25 to 1.75
- gain_merge: float32 [1280], replicated, may hold values from 0.25 to 1.75
- qkv_weight: bfloat16 [1280, 3840], P(None, 'tp'), may hold values from -0.15625 to 0.15625
- out_weight: bfloat16 [1280, 1280], P('tp'), may hold values from -0.15625 to 0.15625
- cotangent: bfloat16 [16384, 5120], P(('grp', 'seq'), 'tp'), may hold values from -0.29882812 to 0.29882812
- patch_counts: int32 [256], P(('grp', 'seq')), may hold values from 64 to 256, as said below
- block_target: int32 [8192], P(('grp', 'seq')), may hold values from 0 to 8191, as said below
Outputs:
- image_rows: bfloat16 [16384, 5120], P(('grp', 'seq'), 'tp')
- grad_qkv: float32 [1280, 3840], P(('grp', 'seq'), 'tp')
- grad_out: float32 [1280, 1280], P('tp', ('grp', 'seq'))
Inputs may be any that keep to these rules, and one draw needn't show every extreme that they name: `patch_counts`: multiples of 4; some image has 256 patches in every draw. `block_target`: each sequence block is named exactly once; the 128 blocks of one owner name exactly 2 blocks of each sequence shard (shard = value // 128).
All inputs are finite; a program needn't handle non-finite values.
Results may differ from a plain program's by a relative error of at most 0.02.
Values may be sent and summed in bfloat16 or wider, within the bound.
A program may use at most 128 MiB of HBM per device.

v0:
```python
import functools

import jax
import jax.numpy as jnp
from jax import lax
from jax.experimental import pallas as pl
from jax.experimental.pallas import tpu as pltpu
from jax.sharding import PartitionSpec as P

HEAD_V = 80
NZ = 8
F32 = jnp.float32
BF16 = jnp.bfloat16
I32 = jnp.int32
MESH = pl.DeviceIdType.MESH


def mm(a, b):
    return lax.dot_general(a, b, (((1,), (0,)), ((), ())), preferred_element_type=F32)


def mm_t(a, b):
    return lax.dot_general(a, b, (((1,), (1,)), ((), ())), preferred_element_type=F32)


def iota(shape, dim):
    return lax.broadcasted_iota(I32, shape, dim)


def ones_where(cond):
    return jnp.where(cond, 1.0, 0.0)


def norm_parts(values):
    center = values - jnp.mean(values, axis=-1, keepdims=True)
    spread = jnp.mean(center * center, axis=-1, keepdims=True)
    return center, lax.rsqrt(spread + 1e-06)


def kernel(
    ny,
    nt,
    n_sems,
    counts,
    x_ref,
    ga_ref,
    gm_ref,
    w_ref,
    ow_ref,
    cot_ref,
    bt_ref,
    image_ref,
    gq_ref,
    go_ref,
    wt,
    nrm,
    nrmt,
    qkvt,
    probs,
    ot,
    hs,
    hm,
    wf,
    res,
    bts,
    btz,
    bty,
    btg,
    placing,
    returning,
    cs,
    cyr,
    czr,
    cgr,
    ms,
    myr,
    mzr,
    mgr,
    inc,
    merged,
    gown,
    gownt,
    ghs,
    ghr,
    ght,
    os_,
    ogr,
    oyr,
    ox,
    oxr,
    oz,
    ozr,
    dws,
    dgr,
    dyr,
    dz,
    dzr,
    ssem,
    rsem,
):
    g = lax.axis_index("grp")
    s = lax.axis_index("seq")
    t = lax.axis_index("tp")
    y = lax.div(s, NZ)
    z = lax.rem(s, NZ)
    images = x_ref.shape[0] // 256
    width = x_ref.shape[1]
    heads = w_ref.shape[1] // (3 * HEAD_V)
    hcols = heads * HEAD_V
    half = width // 2
    yrows = half // ny
    zrows = yrows // NZ

    def at_z(k):
        return lax.rem(z + k, NZ)

    def at_y(k):
        return lax.rem(y + k, ny)

    def at_t(k):
        return lax.rem(t + k, nt)

    def dev_z(k):
        return {"seq": y * NZ + at_z(k)}

    def dev_y(k):
        return {"seq": at_y(k) * NZ + z}

    def dev_t(k):
        return {"tp": at_t(k)}

    dev_g = {"grp": 1 - g}

    used = [0]
    copies = {}

    def push(src, dst, device):
        k = used[0]
        used[0] += 1
        copy = pltpu.make_async_remote_copy(
            src_ref=src,
            dst_ref=dst,
            send_sem=ssem.at[k],
            recv_sem=rsem.at[k],
            device_id=device,
            device_id_type=MESH,
        )
        copy.start()
        copies[id(copy)] = copy
        return copy

    def arrived(group):
        for c in group:
            c.wait_recv()

    def sent(group):
        for c in group:
            c.wait_send()
            del copies[id(c)]

    def rows(start, size):
        return pl.ds(pl.multiple_of(start, size if size & (size - 1) == 0 else 16), size)

    barrier = pltpu.get_barrier_semaphore()
    partners = (
        [dev_z(k) for k in range(1, NZ)]
        + [dev_y(k) for k in range(1, ny)]
        + [dev_t(k) for k in range(1, nt)]
        + [dev_g]
    )
    for device in partners:
        pl.semaphore_signal(barrier, inc=1, device_id=device, device_id_type=MESH)

    eye = ones_where(iota((256, 256), 0) == iota((256, 256), 1)).astype(BF16)

    at = 0
    while at < 3 * hcols:
        size = min(256, 3 * hcols - at)
        wt[at : at + size, :] = mm_t(eye[:size, :size], w_ref[:, at : at + size]).astype(BF16)
        at += size

    bt_row = bt_ref[...]
    bts[...] = jnp.broadcast_to(bt_row, bts.shape)
    pl.semaphore_wait(barrier, len(partners))

    slots_z = [push(bts, btz.at[z], dev_z(k)) for k in range(1, NZ)]
    hrows = hcols // 2
    own_half = pl.ds(pl.multiple_of(g * hrows, 16), hrows)
    weight_t = [push(ow_ref.at[own_half, :], wf.at[t, own_half, :], dev_t(k)) for k in range(1, nt)]
    btz[pl.ds(z, 1)] = bts[...][None]
    wf[pl.ds(t, 1)] = ow_ref[...][None]

    gain_a = ga_ref[...]
    gain_m = gm_ref[...]

    def forward_image(i):
        base = i * 256

        def norm_rows(c, _):
            at = pl.ds(pl.multiple_of(c * 32, 32), 32)
            values = x_ref[pl.ds(pl.multiple_of(base + c * 32, 32), 32), :].astype(F32)
            center, scale = norm_parts(values)
            nrm[at, :] = (center * scale * gain_a).astype(BF16)
            return 0

        lax.fori_loop(0, 8, norm_rows, 0)
        own = ones_where(iota((64, 256), 1) == 4 * iota((64, 256), 0) + t).astype(BF16)
        res[base // 4 : base // 4 + 64, :] = mm(own, x_ref[base : base + 256, :])
        for f in range(width // 256):
            nrmt[f * 256 : (f + 1) * 256, base : base + 256] = mm_t(
                eye, nrm[:, f * 256 : (f + 1) * 256]
            ).astype(BF16)

        def project(c, _):
            at = pl.ds(pl.multiple_of(c * 240, 16), 240)
            qkvt[at, base : base + 256] = mm_t(wt[at, :], nrm[...]).astype(BF16)
            return 0

        lax.fori_loop(0, 3 * hcols // 240, project, 0)
        count = counts[i]
        live = iota((256, 128), 0) < count

        def head(h, _):
            row = h * 3 * HEAD_V
            cols = pl.ds(base, 256)
            k_t = qkvt[pl.ds(pl.multiple_of(row + HEAD_V, 16), HEAD_V), cols]
            v_t = qkvt[pl.ds(pl.multiple_of(row + 2 * HEAD_V, 16), HEAD_V), cols]
            k = mm_t(eye, k_t).astype(BF16)
            for c in range(2):
                q_t = qkvt[pl.ds(pl.multiple_of(row, 16), HEAD_V), pl.ds(base + c * 128, 128)]
                scores = mm(k, q_t) * HEAD_V**-0.5
                scores = jnp.where(live, scores, -1e30)
                weights = jnp.exp(scores - jnp.max(scores, axis=0, keepdims=True))
                weights = weights * (1.0 / jnp.sum(weights, axis=0, keepdims=True))
                weights = weights.astype(BF16)
                probs[i * heads + h, :, c * 128 : (c + 1) * 128] = weights
                ot[pl.ds(pl.multiple_of(h * HEAD_V, 16), HEAD_V), c * 128 : (c + 1) * 128] = mm(
                    v_t, weights
                ).astype(BF16)
            return 0

        lax.fori_loop(0, heads, head, 0)
        by_patch = ones_where(
            iota((256, 256), 1) == 4 * (iota((256, 256), 0) & 63) + (iota((256, 256), 0) >> 6)
        ).astype(BF16)
        hs[i] = mm_t(by_patch, ot[...]).astype(BF16)
        out = pl.ds(i * 64, 64)
        made = [
            push(hs.at[i, rows(at_t(k) * 64, 64), :], hm.at[t, out, :], dev_t(k))
            for k in range(1, nt)
        ]
        hm[pl.ds(t, 1), out, :] = hs[i, rows(t * 64, 64), :][None]
        return made

    row_i, lane_i = iota((256, 256), 0), iota((256, 256), 1)

    def y_to_z():
        return ones_where(
            lane_i == ((row_i >> 3) & (ny - 1)) * 64 + (row_i >> 5) * 8 + (row_i & 7)
        ).astype(BF16)

    def z_to_g():
        return ones_where(
            lane_i
            == ((row_i >> 4) & (NZ - 1)) * 32
            + ((row_i >> 2) & (ny - 1)) * 8
            + (row_i >> 7) * 4
            + (row_i & 3)
        ).astype(BF16)

    def g_to_y():
        return ones_where(
            lane_i
            == ((row_i >> 2) & 1) * 128
            + ((row_i >> 3) & (NZ - 1)) * 16
            + (row_i >> 6) * 4
            + (row_i & 3)
        ).astype(BF16)

    def send_y(buf, dst):
        made = [push(buf.at[rows(at_y(k) * 64, 64), :], dst.at[y], dev_y(k)) for k in range(1, ny)]
        dst[pl.ds(y, 1)] = buf[rows(y * 64, 64), :][None]
        return made

    def send_z(buf, dst):
        made = [push(buf.at[rows(at_z(k) * 32, 32), :], dst.at[z], dev_z(k)) for k in range(1, NZ)]
        dst[pl.ds(z, 1)] = buf[rows(z * 32, 32), :][None]
        return made

    def send_g(buf, dst):
        made = [push(buf.at[rows((1 - g) * 128, 128), :], dst.at[g], dev_g)]
        dst[pl.ds(g, 1)] = buf[rows(g * 128, 128), :][None]
        return made

    heads_in = forward_image(0)
    arrived(slots_z)
    slots_y = [push(btz, bty.at[y], dev_y(k)) for k in range(1, ny)]
    bty[pl.ds(y, 1)] = btz[...][None]

    heads_in += forward_image(1)
    arrived(slots_y)
    slots_g = [push(bty, btg.at[g], dev_g)]
    btg[pl.ds(g, 1)] = bty[...][None]

    pair = iota((256, 128), 0)
    block_lane = iota((256, 128), 1)
    target = jnp.broadcast_to(bt_row, (256, 128)).astype(F32)
    target_of = jnp.sum(jnp.where(block_lane == (pair >> 1), target, 0.0), axis=1, keepdims=True)
    target_of = target_of.astype(I32)
    shard_of = target_of >> 7
    earlier = ((jnp.broadcast_to(bt_row, (256, 128)) >> 7) == shard_of) & (block_lane < (pair >> 1))
    rank_of = jnp.sum(ones_where(earlier), axis=1, keepdims=True).astype(I32)
    row_of = iota((256, 1), 0) & 1
    s_g, s_y, s_z = shard_of >> 5, (shard_of >> 3) & (ny - 1), shard_of & (NZ - 1)
    from_at = s_g * 128 + s_z * 16 + s_y * 4 + rank_of * 2 + row_of
    gathering = ones_where(lane_i == from_at).astype(BF16)
    to_at = (s_y * 64 + s_z * 8 + s_g * 4 + rank_of * 2 + row_of).astype(F32)
    to_row = jnp.sum(jnp.where(row_i == lane_i, to_at, 0.0), axis=0, keepdims=True).astype(I32)
    placing[0] = gathering
    placing[1] = ones_where(row_i == to_row).astype(BF16)

    arrived(slots_g)
    lanes3 = (ny * NZ, 8, 128)
    sub3 = iota(lanes3, 1)
    both = jnp.where(sub3 < 4, btg[0].reshape(lanes3), btg[1].reshape(lanes3))
    hit = (both >> 7) == (g * ny * NZ + s)
    slot = (both & 127).astype(F32)
    lane3 = iota(lanes3, 2).astype(F32)
    first_lane = jnp.min(jnp.where(hit, lane3, 999.0), axis=2, keepdims=True)
    first = lane3 == first_lane
    slot_0 = jnp.sum(jnp.where(hit & first, slot, 0.0), axis=2, keepdims=True)
    slot_1 = jnp.sum(jnp.where(hit & (lane3 != first_lane), slot, 0.0), axis=2, keepdims=True)
    sub1 = iota((ny * NZ, 8, 1), 1)
    slot_row = jnp.where((sub1 & 2) == 2, slot_1, slot_0) * 2.0 + (sub1 & 1).astype(F32)
    slot_row = slot_row.reshape(256, 1)
    pick = ones_where(lane_i.astype(F32) == slot_row)
    slot_lane = jnp.sum(jnp.where(row_i == lane_i, slot_row, 0.0), axis=0, keepdims=True)
    returning[...] = ones_where(row_i.astype(F32) == slot_lane).astype(BF16)

    def moved(order, src, dst):
        for f in range(width // 256):
            cols = slice(f * 256, (f + 1) * 256)
            dst[:, cols] = mm(order, src(cols)).astype(BF16)

    moved(pick.astype(BF16), lambda c: cot_ref[:, c], cs)
    cot_y = send_y(cs, cyr)

    heads_in += forward_image(2)
    arrived(weight_t)
    weight_g = []
    for k in range(1, nt):
        piece = wf.at[at_t(nt - k), own_half, :]
        weight_g.append(push(piece, piece, dev_g))
    arrived(cot_y)
    sent(cot_y)
    moved(y_to_z(), lambda c: cyr[:, :, c].reshape(256, 256), cs)
    cot_z = send_z(cs, czr)

    heads_in += forward_image(3)
    arrived(cot_z)
    sent(cot_z)
    moved(z_to_g(), lambda c: czr[:, :, c].reshape(256, 256), cs)
    cot_g = send_g(cs, cgr)
    arrived(heads_in)
    arrived(weight_g)

    def project_out(c, _):
        cols = pl.ds(pl.multiple_of(c * 256, 256), 256)
        total = res[:, cols]
        for q in range(nt):
            total += mm(hm[q], wf[q, :, cols])
        res[:, cols] = total
        return 0

    lax.fori_loop(0, width // 256, project_out, 0)
    arrived(cot_g)
    moved(placing[0], lambda c: cgr[:, :, c].reshape(256, 256), inc)

    def merge_rows(c, _):
        at = pl.ds(pl.multiple_of(c * 32, 32), 32)
        center, scale = norm_parts(res[at, :])
        hat = center * scale
        alive = ones_where(4 * ((iota((32, 1), 0) + c * 32) & 63) < counts[lax.div(c, 2)])
        merged[at, :] = (hat * gain_m * alive).astype(BF16)
        grad = inc[at, :].astype(F32) * alive * gain_m
        mean_grad = jnp.mean(grad, axis=-1, keepdims=True)
        mean_hat = jnp.mean(grad * hat, axis=-1, keepdims=True)
        gown[at, :] = (scale * (grad - mean_grad - hat * mean_hat)).astype(BF16)
        return 0

    lax.fori_loop(0, 8, merge_rows, 0)

    grads_in = []
    for k in (1, 2, 3, 0):
        q = at_t(k)
        ghs[pl.ds(q, 1)] = mm_t(wf[pl.ds(q, 1)].reshape(hcols, width), gown[...]).astype(BF16)[None]
        if k:
            grads_in.append(push(ghs.at[q], ghr.at[t], dev_t(k)))
        else:
            ghr[pl.ds(q, 1)] = ghs[pl.ds(q, 1)]

    moved(placing[1], lambda c: merged[:, c], ms)
    row_y = send_y(ms, myr)

    for f in range(width // 256):
        gownt[f * 256 : (f + 1) * 256, :] = mm_t(eye, gown[:, f * 256 : (f + 1) * 256]).astype(BF16)

    their_rows = pl.ds(pl.multiple_of((1 - g) * half, 128), half)
    own_rows = pl.ds(pl.multiple_of(g * half, 128), half)

    def out_terms(side):
        def one(q, _):
            for c in range(2):
                at = pl.ds(pl.multiple_of(side * half + c * (half // 2), 64), half // 2)
                os_[q, at, :] = mm(gownt[at, :], hm[q]).astype(BF16)
            return 0

        lax.fori_loop(0, nt, one, 0)

    out_terms(1 - g)
    out_g = [push(os_.at[:, their_rows, :], ogr, dev_g)]
    out_terms(g)

    arrived(grads_in)

    def spread(i, _):
        cols = pl.ds(pl.multiple_of(i * 256, 256), 256)
        total = jnp.zeros((hcols, 256), F32)
        for p in range(nt):
            order = ones_where(lane_i == 4 * (row_i - 64 * i) + p).astype(BF16)
            total += mm(ghr[p], order)
        ght[:, cols] = total.astype(BF16)
        return 0

    lax.fori_loop(0, images, spread, 0)

    def back_head(h):
        row = h * 3 * HEAD_V

        def back_image(i, _):
            cols = pl.ds(pl.multiple_of(i * 256, 256), 256)
            at_q, at_k, at_v = row, row + HEAD_V, row + 2 * HEAD_V
            q_t = qkvt[at_q : at_q + HEAD_V, cols]
            k_t = qkvt[at_k : at_k + HEAD_V, cols]
            v_t = qkvt[at_v : at_v + HEAD_V, cols]
            d_t = ght[h * HEAD_V : (h + 1) * HEAD_V, cols]
            v = mm_t(eye, v_t).astype(BF16)
            weights = probs[i * heads + h]
            grad_v = mm_t(d_t, weights).astype(BF16)
            parts = []
            for c in range(2):
                lanes = slice(c * 128, (c + 1) * 128)
                w = weights[:, lanes].astype(F32)
                grad_w = mm(v, d_t[:, lanes]).astype(BF16).astype(F32)
                inner = jnp.sum(w * grad_w, axis=0, keepdims=True)
                parts.append((w * (grad_w - inner) * HEAD_V**-0.5).astype(BF16))
            grad_s = jnp.concatenate(parts, axis=1)
            grad_q = mm(k_t, grad_s).astype(BF16)
            grad_k = mm_t(q_t, grad_s).astype(BF16)
            qkvt[at_q : at_q + HEAD_V, cols] = grad_q
            qkvt[at_k : at_k + HEAD_V, cols] = grad_k
            qkvt[at_v : at_v + HEAD_V, cols] = grad_v
            return 0

        lax.fori_loop(0, images, back_image, 0)

    def weight_terms(h, side):
        def one(c, _):
            at = pl.ds(pl.multiple_of(side * half + c * (half // 2), 64), half // 2)
            dws[h, at, :] = mm_t(
                nrmt[at, :], qkvt[h * 3 * HEAD_V : (h + 1) * 3 * HEAD_V, :]
            ).astype(BF16)
            return 0

        lax.fori_loop(0, 2, one, 0)

    def to_shards():
        r, c = iota((NZ * 32, yrows), 0), iota((NZ * 32, yrows), 1)
        return ones_where((c == (r >> 5) * zrows + (r & 31)) & ((r & 31) < zrows)).astype(BF16)

    def add(a, b):
        return a.astype(F32) + b.astype(F32)

    def weight_start(h):
        weight_terms(h, 1 - g)
        made = [push(dws.at[h, their_rows, :], dgr.at[h], dev_g)]
        weight_terms(h, g)
        return made

    def weight_y(h, group):
        arrived(group)
        dws[h, own_rows, :] = add(dws[h, own_rows, :], dgr[h]).astype(BF16)
        return [
            push(
                dws.at[h, pl.ds(pl.multiple_of(g * half + at_y(k) * yrows, 16), yrows), :],
                dyr.at[h, k - 1],
                dev_y(k),
            )
            for k in range(1, ny)
        ]

    def weight_z(h, group):
        arrived(group)
        total = dws[h, pl.ds(pl.multiple_of(g * half + y * yrows, 16), yrows), :].astype(F32)
        for k in range(1, ny):
            total += dyr[h, k - 1].astype(F32)
        dz[h] = mm(to_shards(), total.astype(BF16)).astype(BF16)
        return [
            push(dz.at[h, rows(at_z(k) * 32, 32), :], dzr.at[h, k - 1], dev_z(k))
            for k in range(1, NZ)
        ]

    def weight_end(h, group):
        arrived(group)
        total = dz[h, rows(z * 32, 32), :].astype(F32)
        for k in range(1, NZ):
            total += dzr[h, k - 1].astype(F32)
        gq_ref[h] = total

    def out_y(group):
        arrived(group)
        for q in range(nt):
            os_[q, own_rows, :] = add(os_[q, own_rows, :], ogr[q]).astype(BF16)
        return [
            push(
                os_.at[:, pl.ds(pl.multiple_of(g * half + at_y(k) * yrows, 16), yrows), :],
                oyr.at[k - 1],
                dev_y(k),
            )
            for k in range(1, ny)
        ]

    def out_x(group):
        arrived(group)
        mine = pl.ds(pl.multiple_of(g * half + y * yrows, 16), yrows)
        for q in range(nt):
            total = os_[q, mine, :].astype(F32)
            for k in range(1, ny):
                total += oyr[k - 1, q].astype(F32)
            ox[q] = total.astype(BF16)
        return [push(ox.at[at_t(k)], oxr.at[k - 1], dev_t(k)) for k in range(1, nt)]

    def out_z(group):
        arrived(group)
        total = ox[pl.ds(t, 1)].reshape(yrows, hcols).astype(F32)
        for k in range(1, nt):
            total += oxr[k - 1].astype(F32)
        oz[...] = mm(to_shards(), total.astype(BF16)).astype(BF16)
        return [
            push(oz.at[rows(at_z(k) * 32, 32), :], ozr.at[k - 1], dev_z(k)) for k in range(1, NZ)
        ]

    def out_end(group):
        arrived(group)
        total = oz[rows(z * 32, 32), :].astype(F32)
        for k in range(1, NZ):
            total += ozr[k - 1].astype(F32)
        go_ref[...] = total

    back_head(0)
    w0 = weight_start(0)
    o = out_y(out_g)
    arrived(row_y)
    sent(row_y)
    moved(y_to_z(), lambda c: myr[:, :, c].reshape(256, 256), ms)
    row_z = send_z(ms, mzr)

    back_head(1)
    w0 = weight_y(0, w0)
    w1 = weight_start(1)
    o = out_x(o)

    back_head(2)
    w0 = weight_z(0, w0)
    w1 = weight_y(1, w1)
    w2 = weight_start(2)
    o = out_z(o)
    arrived(row_z)
    sent(row_z)
    moved(z_to_g(), lambda c: mzr[:, :, c].reshape(256, 256), ms)
    row_g = send_g(ms, mgr)

    back_head(3)
    w2 = weight_y(2, w2)
    w3 = weight_start(3)
    w1 = weight_z(1, w1)
    weight_end(0, w0)
    w3 = weight_y(3, w3)
    w2 = weight_z(2, w2)
    out_end(o)
    arrived(row_g)
    moved(g_to_y(), lambda c: mgr[:, :, c].reshape(256, 256), inc)
    moved(returning[...], lambda c: inc[:, c], image_ref)
    weight_end(1, w1)
    w3 = weight_z(3, w3)
    weight_end(2, w2)
    weight_end(3, w3)
    for c in copies.values():
        c.wait_send()
    assert used[0] == n_sems


def shards(
    ny, nt, patches_in, gain_attn, gain_merge, qkv_weight, out_weight, cotangent, patch_counts, block_target
):
    row_count, width = patches_in.shape
    images = patch_counts.shape[0]
    hcols = out_weight.shape[0]
    heads = hcols // HEAD_V
    cols = 3 * HEAD_V
    half, yrows = width // 2, width // 2 // ny
    n_sems = (
        (NZ - 1 + ny - 1 + 1)
        + 2 * (nt - 1)
        + images * (nt - 1)
        + 2 * (NZ - 1 + ny - 1 + 1)
        + (nt - 1)
        + (1 + ny - 1 + nt - 1 + NZ - 1)
        + heads * (1 + ny - 1 + NZ - 1)
    )
    v = pltpu.VMEM
    scratch = [
        v((3 * hcols, width), BF16),
        v((256, width), BF16),
        v((width, row_count), BF16),
        v((3 * hcols, row_count), BF16),
        v((images * heads, 256, 256), BF16),
        v((hcols, 256), BF16),
        v((images, 256, hcols), BF16),
        v((nt, 256, hcols), BF16),
        v((nt, hcols, width), BF16),
        v((256, width), F32),
        v((8, 128), I32),
        v((NZ, 8, 128), I32),
        v((ny, NZ, 8, 128), I32),
        v((2, ny, NZ, 8, 128), I32),
        v((2, 256, 256), BF16),
        v((256, 256), BF16),
        v((256, width), BF16),
        v((ny, 64, width), BF16),
        v((NZ, 32, width), BF16),
        v((2, 128, width), BF16),
        v((256, width), BF16),
        v((ny, 64, width), BF16),
        v((NZ, 32, width), BF16),
        v((2, 128, width), BF16),
        v((256, width), BF16),
        v((256, width), BF16),
        v((256, width), BF16),
        v((width, 256), BF16),
        v((nt, hcols, 256), BF16),
        v((nt, hcols, 256), BF16),
        v((hcols, row_count), BF16),
        v((nt, width, hcols), BF16),
        v((nt, half, hcols), BF16),
        v((ny - 1, nt, yrows, hcols), BF16),
        v((nt, yrows, hcols), BF16),
        v((nt - 1, yrows, hcols), BF16),
        v((NZ * 32, hcols), BF16),
        v((NZ - 1, 32, hcols), BF16),
        v((heads, width, cols), BF16),
        v((heads, half, cols), BF16),
        v((heads, ny - 1, yrows, cols), BF16),
        v((heads, NZ * 32, cols), BF16),
        v((heads, NZ - 1, 32, cols), BF16),
        pltpu.SemaphoreType.DMA((n_sems,)),
        pltpu.SemaphoreType.DMA((n_sems,)),
    ]
    in_vmem = pl.BlockSpec(memory_space=pltpu.VMEM)
    image_rows, gq, go = pl.pallas_call(
        functools.partial(kernel, ny, nt, n_sems),
        out_shape=(
            jax.ShapeDtypeStruct((256, width), BF16),
            jax.ShapeDtypeStruct((heads, 32, cols), F32),
            jax.ShapeDtypeStruct((32, hcols), F32),
        ),
        in_specs=[pl.BlockSpec(memory_space=pltpu.SMEM)] + [in_vmem] * 7,
        out_specs=(in_vmem,) * 3,
        scratch_shapes=scratch,
        compiler_params=pltpu.CompilerParams(
            collective_id=0, has_side_effects=True, vmem_limit_bytes=62 << 20
        ),
        name="block",
    )(
        patch_counts,
        patches_in,
        gain_attn.reshape(1, width),
        gain_merge.reshape(1, width),
        qkv_weight,
        out_weight,
        cotangent,
        block_target.reshape(1, -1),
    )
    zrows = yrows // NZ
    grad_qkv = jnp.moveaxis(gq[:, :zrows], 0, 1).reshape(zrows, heads * cols)
    grad_out = go[:zrows].T
    return image_rows, grad_qkv, grad_out


def solution(mesh):
    ny, nt = mesh.shape["seq"] // NZ, mesh.shape["tp"]
    return jax.shard_map(
        functools.partial(shards, ny, nt),
        mesh=mesh,
        in_specs=(
            P(("grp", "seq"), None),
            P(),
            P(),
            P(None, "tp"),
            P("tp", None),
            P(("grp", "seq"), "tp"),
            P(("grp", "seq")),
            P(("grp", "seq")),
        ),
        out_specs=(P(("grp", "seq"), "tp"), P(("grp", "seq"), "tp"), P("tp", ("grp", "seq"))),
        check_vma=False,
    )
```

profile of v0, /device:TPU:1, one launch (start us, length us, event | category | flops | bytes accessed | tf_op | source)
XLA Modules:
  0.0 143.6 jit_solution(7027966559530400256)
XLA Ops:
  0.6 1.3 reshape.18.ga_ref
  1.9 1.3 reshape.19.gm_ref
  3.2 4.5 %copy.12.w_ref = bf16[1280,960]{1,0:T(8,128)(2,1)} copy(bf16[1280,960]{0,1:T(8,128)(2,1)} %param.11) | data formatting | bytes 4915200 | tf_op args[3]
  7.7 130.8 %block.1 = (bf16[256,1280]{1,0:T(8,128)(2,1)}, f32[4,32,240]{2,1,0:T(8,128)}, f32[32,320]{1,0:T(8,128)}) custom-call(s32[4]{0:T(128)} %counts.1, bf16[1024,1280]{1,0:T(8,128)(2,1)} %x_ref.1, f32[1,1280]{1,0:T(1,128)} %reshape.18.ga_ref, f32[1,1280]{1,0:T(1,128)} %reshape.19.gm_ref, bf16[1280,960]{1,0:T(8,128)(2,1)} %copy.12.w_ref, bf16[320,1280]{1,0:T(8,128)(2,1)} %ow_ref.1, ...), custom_call_target="tpu_custom_call" | custom-call | tf_op jit(solution)/shard_map/block/pallas_call | solution.py:670
  138.6 1.4 slice_bitcast_fusion.1
  139.9 0.9 slice_bitcast_fusion
  140.9 0.8 reshape.21
  141.6 2.0 %copy.15 = bf16[256,1280]{1,0:T(8,128)(2,1)} copy(bf16[256,1280]{1,0:T(8,128)(2,1)} %get-tuple-element.12) | data formatting | bytes 1310720
  (1 shorter events, 0.0 us)
where the time goes:
time: 144 us
  Pallas kernels  131 us (91%)
  local copies, waits for them, and re-layouts  12.1 us (8%)
    pallas_call x1, Pallas kernels, shards(): pl.pallas_call(functools.partial(kernel, ny, nt, n_sems), out_shape=(jax....  131 us
    unnamed x2, local copies, waits for them, and re-layouts  6.47 us

commit v1 on v0

v1 whole, which is shorter than its diff:
```python
import functools

import jax
import jax.numpy as jnp
from jax import lax
from jax.experimental import pallas as pl
from jax.experimental.pallas import tpu as pltpu
from jax.sharding import PartitionSpec as P

HEAD_V = 80
NZ = 8
F32 = jnp.float32
BF16 = jnp.bfloat16
I32 = jnp.int32
MESH = pl.DeviceIdType.MESH


def mm(a, b):
    return lax.dot_general(a, b, (((1,), (0,)), ((), ())), preferred_element_type=F32)


def mm_t(a, b):
    return lax.dot_general(a, b, (((1,), (1,)), ((), ())), preferred_element_type=F32)


def iota(shape, dim):
    return lax.broadcasted_iota(I32, shape, dim)


def ones_where(cond):
    return jnp.where(cond, 1.0, 0.0)


def norm_parts(values):
    center = values - jnp.mean(values, axis=-1, keepdims=True)
    spread = jnp.mean(center * center, axis=-1, keepdims=True)
    return center, lax.rsqrt(spread + 1e-06)


def kernel(
    ny,
    nt,
    n_sems,
    counts,
    ga_ref,
    gm_ref,
    bt_ref,
    x_hbm,
    wt_hbm,
    ow_hbm,
    cot_hbm,
    image_ref,
    gq_ref,
    go_ref,
    x_ref,
    wt,
    cot_ref,
    nrm,
    nrmt,
    qkvt,
    probs,
    ot,
    hs,
    hm,
    wf,
    res,
    bts,
    bty,
    btz,
    btg,
    placing,
    returning,
    cs,
    cyr,
    czr,
    cgr,
    ms,
    myr,
    mzr,
    mgr,
    inc,
    merged,
    gown,
    gownt,
    hmt,
    ghs,
    ghr,
    ght,
    oa,
    oag,
    oax,
    oay,
    oayr,
    oaz,
    oazr,
    ob,
    obg,
    obyr,
    obx,
    obxr,
    obz,
    obzr,
    dws,
    dgr,
    dyr,
    dz,
    dzr,
    lsem,
    ssem,
    rsem,
):
    g = lax.axis_index("grp")
    s = lax.axis_index("seq")
    t = lax.axis_index("tp")
    y = lax.div(s, NZ)
    z = lax.rem(s, NZ)
    images = x_ref.shape[0] // 256
    width = x_ref.shape[1]
    hcols = wt.shape[0] // 3
    heads = hcols // HEAD_V
    half = width // 2
    yrows = half // ny
    zrows = yrows // NZ

    def at_z(k):
        return lax.rem(z + k, NZ)

    def at_y(k):
        return lax.rem(y + k, ny)

    def at_t(k):
        return lax.rem(t + k, nt)

    def dev_z(k):
        return {"seq": y * NZ + at_z(k)}

    def dev_y(k):
        return {"seq": at_y(k) * NZ + z}

    def dev_t(k):
        return {"tp": at_t(k)}

    dev_g = {"grp": 1 - g}
    to_t = (1, 3, 2)

    used = [0]
    copies = {}

    def push(src, dst, device):
        k = used[0]
        used[0] += 1
        copy = pltpu.make_async_remote_copy(
            src_ref=src,
            dst_ref=dst,
            send_sem=ssem.at[k],
            recv_sem=rsem.at[k],
            device_id=device,
            device_id_type=MESH,
        )
        copy.start()
        copies[id(copy)] = copy
        return copy

    def arrived(group):
        for c in group:
            c.wait_recv()

    def sent(group):
        for c in group:
            c.wait_send()
            del copies[id(c)]

    def rows(start, size):
        return pl.ds(pl.multiple_of(start, size if size & (size - 1) == 0 else 16), size)

    barrier = pltpu.get_barrier_semaphore()
    partners = (
        [dev_z(k) for k in range(1, NZ)]
        + [dev_y(k) for k in range(1, ny)]
        + [dev_t(k) for k in range(1, nt)]
        + [dev_g]
    )
    for device in partners:
        pl.semaphore_signal(barrier, inc=1, device_id=device, device_id_type=MESH)

    def image_rows_of(i):
        at = pl.ds(i * 256, 256)
        return pltpu.make_async_copy(x_hbm.at[at, :], x_ref.at[at, :], lsem.at[i])

    loads_x = [image_rows_of(i) for i in range(images)]
    load_w = pltpu.make_async_copy(wt_hbm, wt, lsem.at[images])
    load_c = pltpu.make_async_copy(cot_hbm, cot_ref, lsem.at[images + 1])
    load_o = pltpu.make_async_copy(ow_hbm, wf.at[t], lsem.at[images + 2])
    loads_x[0].start()
    load_w.start()
    load_c.start()

    eye = ones_where(iota((256, 256), 0) == iota((256, 256), 1)).astype(BF16)
    bt_row = bt_ref[...]
    bts[...] = jnp.broadcast_to(bt_row, bts.shape)
    pl.semaphore_wait(barrier, len(partners))

    slots_y = [push(bts, bty.at[y], dev_y(k)) for k in range(1, ny)]
    hrows = hcols // 2
    own_half = pl.ds(pl.multiple_of(g * hrows, 16), hrows)
    weight_t = [
        push(ow_hbm.at[own_half, :], wf.at[t, own_half, :], dev_t(k)) for k in range(1, nt)
    ]
    for load in loads_x[1:]:
        load.start()
    load_o.start()
    bty[pl.ds(y, 1)] = bts[...][None]

    gain_a = ga_ref[...].reshape(1, width)
    gain_m = gm_ref[...].reshape(1, width)

    def forward_norm(i):
        base = i * 256
        loads_x[i].wait()

        def norm_rows(c, _):
            at = pl.ds(pl.multiple_of(c * 32, 32), 32)
            values = x_ref[pl.ds(pl.multiple_of(base + c * 32, 32), 32), :].astype(F32)
            center, scale = norm_parts(values)
            nrm[at, :] = (center * scale * gain_a).astype(BF16)
            return 0

        lax.fori_loop(0, 8, norm_rows, 0)
        own = ones_where(iota((64, 256), 1) == 4 * iota((64, 256), 0) + t).astype(BF16)
        res[base // 4 : base // 4 + 64, :] = mm(own, x_ref[base : base + 256, :])
        for f in range(width // 256):
            nrmt[f * 256 : (f + 1) * 256, base : base + 256] = mm_t(
                eye, nrm[:, f * 256 : (f + 1) * 256]
            ).astype(BF16)

    def forward_qkv(i):
        base = i * 256
        if i == 0:
            load_w.wait()

        def project(c, _):
            at = pl.ds(pl.multiple_of(c * 240, 16), 240)
            qkvt[at, base : base + 256] = mm_t(wt[at, :], nrm[...]).astype(BF16)
            return 0

        lax.fori_loop(0, 3 * hcols // 240, project, 0)

    def forward_attend(i):
        base = i * 256
        live = iota((256, 128), 0) < counts[i]
        cols = pl.ds(base, 256)
        for h in range(heads):
            row = h * 3 * HEAD_V
            k = mm_t(eye, qkvt[row + HEAD_V : row + 2 * HEAD_V, cols]).astype(BF16)
            v_t = qkvt[row + 2 * HEAD_V : row + 3 * HEAD_V, cols]
            for c in range(2):
                lanes = slice(c * 128, (c + 1) * 128)
                q_t = qkvt[row : row + HEAD_V, pl.ds(base + c * 128, 128)]
                scores = mm(k, q_t) * HEAD_V**-0.5
                scores = jnp.where(live, scores, -1e30)
                weights = jnp.exp(scores - jnp.max(scores, axis=0, keepdims=True))
                weights = weights * (1.0 / jnp.sum(weights, axis=0, keepdims=True))
                weights = weights.astype(BF16)
                probs[i * heads + h, :, lanes] = weights
                ot[h * HEAD_V : (h + 1) * HEAD_V, lanes] = mm(v_t, weights).astype(BF16)
        by_patch = ones_where(
            iota((256, 256), 1) == 4 * (iota((256, 256), 0) & 63) + (iota((256, 256), 0) >> 6)
        ).astype(BF16)
        hs[i] = mm_t(by_patch, ot[...]).astype(BF16)
        out = pl.ds(i * 64, 64)
        made = [
            push(hs.at[i, rows(at_t(k) * 64, 64), :], hm.at[t, out, :], dev_t(k)) for k in to_t
        ]
        hm[pl.ds(t, 1), out, :] = hs[i, rows(t * 64, 64), :][None]
        return made

    row_i, lane_i = iota((256, 256), 0), iota((256, 256), 1)

    def z_to_y():
        return ones_where(
            lane_i == ((row_i >> 3) & (NZ - 1)) * 32 + (row_i >> 6) * 8 + (row_i & 7)
        ).astype(BF16)

    def y_to_g():
        return ones_where(
            lane_i
            == ((row_i >> 5) & (ny - 1)) * 64
            + ((row_i >> 2) & (NZ - 1)) * 8
            + (row_i >> 7) * 4
            + (row_i & 3)
        ).astype(BF16)

    def g_to_z():
        return ones_where(
            lane_i
            == ((row_i >> 2) & 1) * 128
            + ((row_i >> 3) & (ny - 1)) * 32
            + (row_i >> 5) * 4
            + (row_i & 3)
        ).astype(BF16)

    def send_y(buf, dst):
        made = [push(buf.at[rows(at_y(k) * 64, 64), :], dst.at[y], dev_y(k)) for k in (1, 3, 2)]
        dst[pl.ds(y, 1)] = buf[rows(y * 64, 64), :][None]
        return made

    def send_z(buf, dst):
        made = [
            push(buf.at[rows(at_z(k) * 32, 32), :], dst.at[z], dev_z(k))
            for k in (4, 3, 5, 2, 6, 1, 7)
        ]
        dst[pl.ds(z, 1)] = buf[rows(z * 32, 32), :][None]
        return made

    def send_g(buf, dst):
        made = [push(buf.at[rows((1 - g) * 128, 128), :], dst.at[g], dev_g)]
        dst[pl.ds(g, 1)] = buf[rows(g * 128, 128), :][None]
        return made

    def moved(order, src, dst):
        for f in range(width // 256):
            cols = slice(f * 256, (f + 1) * 256)
            dst[:, cols] = mm(order, src(cols)).astype(BF16)

    forward_norm(0)
    arrived(slots_y)
    slots_z = [push(bty, btz.at[z], dev_z(k)) for k in range(1, NZ)]
    btz[pl.ds(z, 1)] = bty[...][None]
    forward_qkv(0)
    arrived(slots_z)
    slots_g = [push(btz, btg.at[g], dev_g)]
    btg[pl.ds(g, 1)] = btz[...][None]

    pair = iota((256, 128), 0)
    block_lane = iota((256, 128), 1)
    target = jnp.broadcast_to(bt_row, (256, 128)).astype(F32)
    target_of = jnp.sum(jnp.where(block_lane == (pair >> 1), target, 0.0), axis=1, keepdims=True)
    target_of = target_of.astype(I32)
    shard_of = target_of >> 7
    earlier = ((jnp.broadcast_to(bt_row, (256, 128)) >> 7) == shard_of) & (block_lane < (pair >> 1))
    rank_of = jnp.sum(ones_where(earlier), axis=1, keepdims=True).astype(I32)
    row_of = rank_of * 2 + (iota((256, 1), 0) & 1)
    s_g, s_y, s_z = shard_of >> 5, (shard_of >> 3) & (ny - 1), shard_of & (NZ - 1)
    placing[0] = ones_where(lane_i == shard_of * 4 + row_of).astype(BF16)
    to_at = (s_z * 32 + s_y * 8 + s_g * 4 + row_of).astype(F32)
    to_row = jnp.sum(jnp.where(row_i == lane_i, to_at, 0.0), axis=0, keepdims=True).astype(I32)
    placing[1] = ones_where(row_i == to_row).astype(BF16)

    arrived(slots_g)
    lanes3 = (ny * NZ, 8, 128)
    sub3 = iota(lanes3, 1)
    both = jnp.where(sub3 < 4, btg[0].reshape(lanes3), btg[1].reshape(lanes3))
    hit = (both >> 7) == (g * ny * NZ + s)
    slot = (both & 127).astype(F32)
    lane3 = iota(lanes3, 2).astype(F32)
    first_lane = jnp.min(jnp.where(hit, lane3, 999.0), axis=2, keepdims=True)
    slot_0 = jnp.sum(jnp.where(hit & (lane3 == first_lane), slot, 0.0), axis=2, keepdims=True)
    slot_1 = jnp.sum(jnp.where(hit & (lane3 != first_lane), slot, 0.0), axis=2, keepdims=True)
    sub1 = iota((ny * NZ, 8, 1), 1)
    slot_row = jnp.where((sub1 & 2) == 2, slot_1, slot_0) * 2.0 + (sub1 & 1).astype(F32)
    slot_row = slot_row.reshape(256, 1)
    pick = ones_where(lane_i.astype(F32) == slot_row).astype(BF16)
    load_c.wait()
    moved(pick, lambda c: cot_ref[:, c], cs)
    cot_z = send_z(cs, czr)

    heads_in = forward_attend(0)
    slot_lane = jnp.sum(jnp.where(row_i == lane_i, slot_row, 0.0), axis=0, keepdims=True)
    back_at = ones_where(row_i.astype(F32) == slot_lane).astype(BF16)
    returning[...] = mm(back_at, g_to_z()).astype(BF16)

    forward_norm(1)
    forward_qkv(1)
    heads_in += forward_attend(1)
    forward_norm(2)
    forward_qkv(2)
    heads_in += forward_attend(2)
    arrived(cot_z)
    sent(cot_z)
    moved(z_to_y(), lambda c: czr[:, :, c].reshape(256, 256), cs)
    cot_y = send_y(cs, cyr)
    arrived(weight_t)
    weight_g = []
    for k in range(1, nt):
        piece = wf.at[at_t(nt - k), own_half, :]
        weight_g.append(push(piece, piece, dev_g))
    forward_norm(3)
    forward_qkv(3)
    heads_in += forward_attend(3)
    arrived(cot_y)
    sent(cot_y)
    moved(y_to_g(), lambda c: cyr[:, :, c].reshape(256, 256), cs)
    cot_g = send_g(cs, cgr)
    load_o.wait()
    arrived(heads_in)
    arrived(weight_g)

    def project_out(c, _):
        cols = pl.ds(pl.multiple_of(c * 256, 256), 256)
        total = res[:, cols]
        for q in range(nt):
            total += mm(hm[q], wf[q, :, cols])
        res[:, cols] = total
        return 0

    lax.fori_loop(0, width // 256, project_out, 0)
    arrived(cot_g)
    moved(placing[0], lambda c: cgr[:, :, c].reshape(256, 256), inc)

    def merge_rows(c, _):
        at = pl.ds(pl.multiple_of(c * 32, 32), 32)
        center, scale = norm_parts(res[at, :])
        hat = center * scale
        alive = ones_where(4 * ((iota((32, 1), 0) + c * 32) & 63) < counts[lax.div(c, 2)])
        merged[at, :] = (hat * gain_m * alive).astype(BF16)
        grad = inc[at, :].astype(F32) * alive * gain_m
        mean_grad = jnp.mean(grad, axis=-1, keepdims=True)
        mean_hat = jnp.mean(grad * hat, axis=-1, keepdims=True)
        gown[at, :] = (scale * (grad - mean_grad - hat * mean_hat)).astype(BF16)
        return 0

    lax.fori_loop(0, 8, merge_rows, 0)

    pairs = 2
    prows = hcols // pairs
    for k in to_t + (0,):
        q = at_t(k)
        ghs[pl.ds(q, 1)] = mm_t(wf[pl.ds(q, 1)].reshape(hcols, width), gown[...]).astype(BF16)[None]
    grads_in = [
        [
            push(
                ghs.at[at_t(k), pl.ds(j * prows, prows), :],
                ghr.at[t, pl.ds(j * prows, prows), :],
                dev_t(k),
            )
            for k in to_t
        ]
        for j in range(pairs)
    ]
    ghr[pl.ds(t, 1)] = ghs[pl.ds(t, 1)]

    moved(placing[1], lambda c: merged[:, c], ms)
    row_z = send_z(ms, mzr)

    for f in range(width // 256):
        gownt[f * 256 : (f + 1) * 256, :] = mm_t(eye, gown[:, f * 256 : (f + 1) * 256]).astype(BF16)
    wide = hcols - 128
    for q in range(nt):
        hmt[q] = mm_t(eye[:wide, :wide], hm[q, :, 128:]).astype(BF16)

    def terms_b(side):
        def one(c, _):
            at = pl.ds(pl.multiple_of(side * half + c * (half // 2), 64), half // 2)
            to = pl.ds(pl.multiple_of(c * (half // 2), 64), half // 2)
            for q in range(nt):
                ob[pl.ds(side, 1), to, q * 128 : (q + 1) * 128] = mm(
                    gownt[at, :], hm[q, :, :128]
                ).astype(BF16)[None]
            return 0

        lax.fori_loop(0, 2, one, 0)

    def terms_a(side, k):
        cols = pl.ds(pl.multiple_of(side * half, 128), half)
        q = at_t(k)
        value = mm(hmt[pl.ds(q, 1)].reshape(wide, 256), gown[:, cols])
        oa[pl.ds(side, 1), pl.ds(q, 1)] = value.astype(BF16)[None, None]

    terms_b(1 - g)
    b_g = [push(ob.at[1 - g], obg, dev_g)]
    a_g = []
    for k in to_t + (0,):
        terms_a(1 - g, k)
        a_g.append([push(oa.at[1 - g, at_t(k)], oag.at[at_t(k)], dev_g)])
    terms_b(g)
    for k in to_t + (0,):
        terms_a(g, k)

    def spread(j):
        def one(i, _):
            cols = pl.ds(pl.multiple_of(i * 256, 256), 256)
            total = jnp.zeros((prows, 256), F32)
            for p in range(nt):
                order = ones_where(lane_i == 4 * (row_i - 64 * i) + p).astype(BF16)
                total += mm(ghr[p, j * prows : (j + 1) * prows, :], order)
            ght[j * prows : (j + 1) * prows, cols] = total.astype(BF16)
            return 0

        lax.fori_loop(0, images, one, 0)

    def back_head(h):
        row = h * 3 * HEAD_V

        def back_image(i, _):
            cols = pl.ds(pl.multiple_of(i * 256, 256), 256)
            at_q, at_k, at_v = row, row + HEAD_V, row + 2 * HEAD_V
            q_t = qkvt[at_q : at_q + HEAD_V, cols]
            k_t = qkvt[at_k : at_k + HEAD_V, cols]
            v_t = qkvt[at_v : at_v + HEAD_V, cols]
            d_t = ght[h * HEAD_V : (h + 1) * HEAD_V, cols]
            v = mm_t(eye, v_t).astype(BF16)
            weights = probs[i * heads + h]
            grad_v = mm_t(d_t, weights).astype(BF16)
            parts = []
            for c in range(2):
                lanes = slice(c * 128, (c + 1) * 128)
                w = weights[:, lanes].astype(F32)
                grad_w = mm(v, d_t[:, lanes]).astype(BF16).astype(F32)
                inner = jnp.sum(w * grad_w, axis=0, keepdims=True)
                parts.append((w * (grad_w - inner) * HEAD_V**-0.5).astype(BF16))
            grad_s = jnp.concatenate(parts, axis=1)
            grad_q = mm(k_t, grad_s).astype(BF16)
            grad_k = mm_t(q_t, grad_s).astype(BF16)
            qkvt[at_q : at_q + HEAD_V, cols] = grad_q
            qkvt[at_k : at_k + HEAD_V, cols] = grad_k
            qkvt[at_v : at_v + HEAD_V, cols] = grad_v
            return 0

        lax.fori_loop(0, images, back_image, 0)

    def weight_terms(h, side):
        def one(c, _):
            at = pl.ds(pl.multiple_of(side * half + c * (half // 2), 64), half // 2)
            dws[h, at, :] = mm_t(
                nrmt[at, :], qkvt[h * 3 * HEAD_V : (h + 1) * 3 * HEAD_V, :]
            ).astype(BF16)
            return 0

        lax.fori_loop(0, 2, one, 0)

    def to_shards():
        r, c = iota((NZ * 32, yrows), 0), iota((NZ * 32, yrows), 1)
        return ones_where((c == (r >> 5) * zrows + (r & 31)) & ((r & 31) < zrows)).astype(BF16)

    def add(a, b):
        return a.astype(F32) + b.astype(F32)

    their_rows = pl.ds(pl.multiple_of((1 - g) * half, 128), half)
    own_rows = pl.ds(pl.multiple_of(g * half, 128), half)
    order_y = [(k, k - 1) for k in (1, 3, 2)]
    order_z = [(k, k - 1) for k in (4, 3, 5, 2, 6, 1, 7)]

    def rows_y(k):
        return pl.ds(pl.multiple_of(at_y(k) * yrows, 16), yrows)

    def weight_start(h):
        weight_terms(h, 1 - g)
        made = [push(dws.at[h, their_rows, :], dgr.at[h], dev_g)]
        weight_terms(h, g)
        return made

    def weight_y(h, group):
        arrived(group)
        dgr[h] = add(dws[h, own_rows, :], dgr[h]).astype(BF16)
        return [push(dgr.at[h, rows_y(k), :], dyr.at[h, j], dev_y(k)) for k, j in order_y]

    def weight_z(h, group):
        arrived(group)
        total = dgr[h, rows_y(0), :].astype(F32)
        for k in range(1, ny):
            total += dyr[h, k - 1].astype(F32)
        dz[h] = mm(to_shards(), total.astype(BF16)).astype(BF16)
        return [
            push(dz.at[h, rows(at_z(k) * 32, 32), :], dzr.at[h, j], dev_z(k)) for k, j in order_z
        ]

    def weight_end(h, group):
        arrived(group)
        total = dz[h, rows(z * 32, 32), :].astype(F32)
        for k in range(1, NZ):
            total += dzr[h, k - 1].astype(F32)
        gq_ref[h] = total

    def b_y(group):
        arrived(group)
        obg[...] = add(ob[pl.ds(g, 1)].reshape(half, nt * 128), obg[...]).astype(BF16)
        return [push(obg.at[rows_y(k), :], obyr.at[j], dev_y(k)) for k, j in order_y]

    def b_x(group):
        arrived(group)
        total = obg[rows_y(0), :].astype(F32)
        for k in range(1, ny):
            total += obyr[k - 1].astype(F32)
        for q in range(nt):
            obx[q] = total[:, q * 128 : (q + 1) * 128].astype(BF16)
        return [push(obx.at[at_t(k)], obxr.at[k - 1], dev_t(k)) for k in to_t]

    def b_z(group):
        arrived(group)
        total = obx[pl.ds(t, 1)].reshape(yrows, 128).astype(F32)
        for k in range(1, nt):
            total += obxr[k - 1].astype(F32)
        obz[...] = mm(to_shards(), total.astype(BF16)).astype(BF16)
        return [push(obz.at[rows(at_z(k) * 32, 32), :], obzr.at[j], dev_z(k)) for k, j in order_z]

    def b_end(group):
        arrived(group)
        total = obz[rows(z * 32, 32), :].astype(F32)
        for k in range(1, NZ):
            total += obzr[k - 1].astype(F32)
        go_ref[:, :128] = total

    def a_x(groups):
        made = []
        for k, group in zip(to_t + (0,), groups):
            arrived(group)
            q = at_t(k)
            mine = oa[pl.ds(g, 1), pl.ds(q, 1)].reshape(wide, half)
            oag[pl.ds(q, 1)] = add(mine, oag[pl.ds(q, 1)].reshape(wide, half)).astype(BF16)[None]
            if k:
                made.append(push(oag.at[q], oax.at[k - 1], dev_t(k)))
        return made

    def a_y(group):
        arrived(group)
        for f in range(half // 128):
            cols = slice(f * 128, (f + 1) * 128)
            total = oag[pl.ds(t, 1), :, cols].reshape(wide, 128).astype(F32)
            for k in range(1, nt):
                total += oax[k - 1, :, cols].astype(F32)
            oay[cols, :] = mm_t(eye[:128, :128], total.astype(BF16)).astype(BF16)
        return [push(oay.at[rows_y(k), :], oayr.at[j], dev_y(k)) for k, j in order_y]

    def a_z(group):
        arrived(group)
        total = oay[rows_y(0), :].astype(F32)
        for k in range(1, ny):
            total += oayr[k - 1].astype(F32)
        oaz[...] = mm(to_shards(), total.astype(BF16)).astype(BF16)
        return [push(oaz.at[rows(at_z(k) * 32, 32), :], oazr.at[j], dev_z(k)) for k, j in order_z]

    def a_end(group):
        arrived(group)
        total = oaz[rows(z * 32, 32), :].astype(F32)
        for k in range(1, NZ):
            total += oazr[k - 1].astype(F32)
        go_ref[:, 128:] = total

    arrived(grads_in[0])
    spread(0)
    back_head(0)
    b = b_y(b_g)
    a = a_x(a_g)
    w0 = weight_start(0)
    back_head(1)
    w0 = weight_y(0, w0)
    w1 = weight_start(1)
    arrived(grads_in[1])
    spread(1)
    back_head(2)
    w1 = weight_y(1, w1)
    w2 = weight_start(2)
    arrived(row_z)
    sent(row_z)
    moved(z_to_y(), lambda c: mzr[:, :, c].reshape(256, 256), ms)
    row_y = send_y(ms, myr)
    w0 = weight_z(0, w0)
    b = b_x(b)
    back_head(3)
    w2 = weight_y(2, w2)
    w3 = weight_start(3)
    w1 = weight_z(1, w1)
    w3 = weight_y(3, w3)
    b = b_z(b)
    a = a_y(a)
    w2 = weight_z(2, w2)
    arrived(row_y)
    sent(row_y)
    moved(y_to_g(), lambda c: myr[:, :, c].reshape(256, 256), ms)
    row_g = send_g(ms, mgr)
    weight_end(0, w0)
    w3 = weight_z(3, w3)
    a = a_z(a)
    weight_end(1, w1)
    b_end(b)
    arrived(row_g)
    moved(returning[...], lambda c: mgr[:, :, c].reshape(256, 256), image_ref)
    weight_end(2, w2)
    weight_end(3, w3)
    a_end(a)
    for c in copies.values():
        c.wait_send()
    assert used[0] == n_sems


def shards(
    ny, nt, patches_in, gain_attn, gain_merge, qkv_weight, out_weight, cotangent, patch_counts, block_target
):
    row_count, width = patches_in.shape
    images = patch_counts.shape[0]
    hcols = out_weight.shape[0]
    heads = hcols // HEAD_V
    cols = 3 * HEAD_V
    half, yrows = width // 2, width // 2 // ny
    wide = hcols - 128
    to_all = NZ - 1 + ny - 1 + 1
    n_sems = (
        to_all
        + 2 * (nt - 1)
        + images * (nt - 1)
        + 2 * to_all
        + 2 * (nt - 1)
        + to_all + nt - 1
        + to_all + 2 * nt - 2
        + heads * to_all
    )
    v = pltpu.VMEM
    scratch = [
        v((row_count, width), BF16),
        v((3 * hcols, width), BF16),
        v((256, width), BF16),
        v((256, width), BF16),
        v((width, row_count), BF16),
        v((3 * hcols, row_count), BF16),
        v((images * heads, 256, 256), BF16),
        v((hcols, 256), BF16),
        v((images, 256, hcols), BF16),
        v((nt, 256, hcols), BF16),
        v((nt, hcols, width), BF16),
        v((256, width), F32),
        v((8, 128), I32),
        v((ny, 8, 128), I32),
        v((NZ, ny, 8, 128), I32),
        v((2, NZ, ny, 8, 128), I32),
        v((2, 256, 256), BF16),
        v((256, 256), BF16),
        v((256, width), BF16),
        v((ny, 64, width), BF16),
        v((NZ, 32, width), BF16),
        v((2, 128, width), BF16),
        v((256, width), BF16),
        v((ny, 64, width), BF16),
        v((NZ, 32, width), BF16),
        v((2, 128, width), BF16),
        v((256, width), BF16),
        v((256, width), BF16),
        v((256, width), BF16),
        v((width, 256), BF16),
        v((nt, wide, 256), BF16),
        v((nt, hcols, 256), BF16),
        v((nt, hcols, 256), BF16),
        v((hcols, row_count), BF16),
        v((2, nt, wide, half), BF16),
        v((nt, wide, half), BF16),
        v((nt - 1, wide, half), BF16),
        v((half, wide), BF16),
        v((ny - 1, yrows, wide), BF16),
        v((NZ * 32, wide), BF16),
        v((NZ - 1, 32, wide), BF16),
        v((2, half, nt * 128), BF16),
        v((half, nt * 128), BF16),
        v((ny - 1, yrows, nt * 128), BF16),
        v((nt, yrows, 128), BF16),
        v((nt - 1, yrows, 128), BF16),
        v((NZ * 32, 128), BF16),
        v((NZ - 1, 32, 128), BF16),
        v((heads, width, cols), BF16),
        v((heads, half, cols), BF16),
        v((heads, ny - 1, yrows, cols), BF16),
        v((heads, NZ * 32, cols), BF16),
        v((heads, NZ - 1, 32, cols), BF16),
        pltpu.SemaphoreType.DMA((images + 3,)),
        pltpu.SemaphoreType.DMA((n_sems,)),
        pltpu.SemaphoreType.DMA((n_sems,)),
    ]
    in_vmem = pl.BlockSpec(memory_space=pltpu.VMEM)
    in_hbm = pl.BlockSpec(memory_space=pl.ANY)
    image_rows, gq, go = pl.pallas_call(
        functools.partial(kernel, ny, nt, n_sems),
        out_shape=(
            jax.ShapeDtypeStruct((256, width), BF16),
            jax.ShapeDtypeStruct((heads, 32, cols), F32),
            jax.ShapeDtypeStruct((32, hcols), F32),
        ),
        in_specs=[pl.BlockSpec(memory_space=pltpu.SMEM)] + [in_vmem] * 3 + [in_hbm] * 4,
        out_specs=(in_vmem,) * 3,
        scratch_shapes=scratch,
        compiler_params=pltpu.CompilerParams(
            collective_id=0, has_side_effects=True, vmem_limit_bytes=62 << 20
        ),
        name="block",
    )(
        patch_counts,
        gain_attn,
        gain_merge,
        block_target.reshape(1, -1),
        patches_in,
        qkv_weight.T,
        out_weight,
        cotangent,
    )
    zrows = yrows // NZ
    grad_qkv = jnp.moveaxis(gq[:, :zrows], 0, 1).reshape(zrows, heads * cols)
    grad_out = go[:zrows].T
    return image_rows, grad_qkv, grad_out


def solution(mesh):
    ny, nt = mesh.shape["seq"] // NZ, mesh.shape["tp"]
    return jax.shard_map(
        functools.partial(shards, ny, nt),
        mesh=mesh,
        in_specs=(
            P(("grp", "seq"), None),
            P(),
            P(),
            P(None, "tp"),
            P("tp", None),
            P(("grp", "seq"), "tp"),
            P(("grp", "seq")),
            P(("grp", "seq")),
        ),
        out_specs=(P(("grp", "seq"), "tp"), P(("grp", "seq"), "tp"), P("tp", ("grp", "seq"))),
        check_vma=False,
    )
```

time: 144 us -> 113 us (0.78)
  Pallas kernels: 131 us -> 107 us
  local copies, waits for them, and re-layouts: 12.1 us -> 5.04 us
    pallas_call x1, Pallas kernels: 131 us -> 107 us  [shards(): pl.pallas_call(functools.partial(kernel, ny, nt, n_sems), out_shape=(jax....]
    unnamed x2 -> x1, local copies, waits for them, and re-layouts: 6.47 us -> 1.96 us
    reshape x2 -> x0, local copies, waits for them, and re-layouts: 2.59 us -> none  [the longest x1 1.29 us: shards(): gain_attn.reshape(1, width)]
where the time goes in v1:
time: 113 us; the launch traced here: 112 us
  Pallas kernels  107 us (95%)
  local copies, waits for them, and re-layouts  5.04 us (4%)
    pallas_call x1, Pallas kernels, shards(): pl.pallas_call(functools.partial(kernel, ny, nt, n_sems), out_shape=(jax....  107 us

profile of v1, /device:TPU:1, one launch (start us, length us, event | category | flops | bytes accessed | tf_op | source)
XLA Modules:
  0.0 112.4 jit_solution(8693521207411410075)
XLA Ops:
  0.6 106.7 %block.1 = (bf16[256,1280]{1,0:T(8,128)(2,1)}, f32[4,32,240]{2,1,0:T(8,128)}, f32[32,320]{1,0:T(8,128)}) custom-call(s32[4]{0:T(128)} %counts.1, f32[1280]{0:T(1024)} %ga_ref.1, f32[1280]{0:T(1024)} %gm_ref.1, s32[1,128]{1,0:T(1,128)} %bitcast.7, bf16[1024,1280]{1,0:T(8,128)(2,1)} %x_hbm.1, bf16[960,1280]{1,0:T(8,128)(2,1)} %bitcast.6, ...), custom_call_target="tpu_custom_call" | custom-call | tf_op jit(solution)/shard_map/block/pallas_call | solution.py:768
  107.3 1.4 %slice_bitcast_fusion.1 = f32[320,20]{0,1:T(8,128)} fusion(f32[32,320]{1,0:T(8,128)} %get-tuple-element.8), kind=kLoop, calls=%fused_computation.1 | loop fusion | bytes 51200 | tf_op jit(solution)/shard_map/transpose | solution.py:794
  108.7 0.9 slice_bitcast_fusion
  109.6 0.8 reshape.13
  110.4 2.0 %copy.13 = bf16[256,1280]{1,0:T(8,128)(2,1)} copy(bf16[256,1280]{1,0:T(8,128)(2,1)} %get-tuple-element.12) | data formatting | bytes 1310720
  (1 shorter events, 0.0 us)

commit v2 on v1

--- a/solution.py
+++ b/solution.py
@@ -49,7 +49,7 @@
     wt_hbm,
     ow_hbm,
     cot_hbm,
-    image_ref,
+    image_hbm,
     gq_ref,
     go_ref,
     x_ref,
@@ -79,6 +79,7 @@
     mzr,
     mgr,
     inc,
+    image,
     merged,
     gown,
     gownt,
@@ -144,31 +145,41 @@
     to_t = (1, 3, 2)
 
     used = [0]
-    copies = {}
-
-    def push(src, dst, device):
-        k = used[0]
-        used[0] += 1
-        copy = pltpu.make_async_remote_copy(
-            src_ref=src,
-            dst_ref=dst,
-            send_sem=ssem.at[k],
-            recv_sem=rsem.at[k],
-            device_id=device,
-            device_id_type=MESH,
-        )
-        copy.start()
-        copies[id(copy)] = copy
-        return copy
-
-    def arrived(group):
-        for c in group:
-            c.wait_recv()
-
-    def sent(group):
-        for c in group:
-            c.wait_send()
-            del copies[id(c)]
+    open_sends = {}
+
+    class Group:
+        def __init__(self, whole):
+            self.k = used[0]
+            used[0] += 1
+            self.whole = self.copy(whole, whole, dev_g)
+            open_sends[self.k] = self
+
+        def copy(self, src, dst, device):
+            return pltpu.make_async_remote_copy(
+                src_ref=src,
+                dst_ref=dst,
+                send_sem=ssem.at[self.k],
+                recv_sem=rsem.at[self.k],
+                device_id=device,
+                device_id_type=MESH,
+            )
+
+        def push(self, src, dst, device):
+            self.copy(src, dst, device).start()
+            return self
+
+        def arrived(self):
+            self.whole.wait_recv()
+
+        def sent(self):
+            self.whole.wait_send()
+            del open_sends[self.k]
+
+    def push_all(whole, pieces):
+        group = Group(whole)
+        for piece in pieces:
+            group.push(*piece)
+        return group
 
     def rows(start, size):
         return pl.ds(pl.multiple_of(start, size if size & (size - 1) == 0 else 16), size)
@@ -195,22 +206,14 @@
     load_w.start()
     load_c.start()
 
+    for load in loads_x[1:]:
+        load.start()
+    load_o.start()
+    hrows = hcols // 2
+    own_half = pl.ds(pl.multiple_of(g * hrows, 16), hrows)
     eye = ones_where(iota((256, 256), 0) == iota((256, 256), 1)).astype(BF16)
     bt_row = bt_ref[...]
     bts[...] = jnp.broadcast_to(bt_row, bts.shape)
-    pl.semaphore_wait(barrier, len(partners))
-
-    slots_y = [push(bts, bty.at[y], dev_y(k)) for k in range(1, ny)]
-    hrows = hcols // 2
-    own_half = pl.ds(pl.multiple_of(g * hrows, 16), hrows)
-    weight_t = [
-        push(ow_hbm.at[own_half, :], wf.at[t, own_half, :], dev_t(k)) for k in range(1, nt)
-    ]
-    for load in loads_x[1:]:
-        load.start()
-    load_o.start()
-    bty[pl.ds(y, 1)] = bts[...][None]
-
     gain_a = ga_ref[...].reshape(1, width)
     gain_m = gm_ref[...].reshape(1, width)
 
@@ -267,12 +270,12 @@
             iota((256, 256), 1) == 4 * (iota((256, 256), 0) & 63) + (iota((256, 256), 0) >> 6)
         ).astype(BF16)
         hs[i] = mm_t(by_patch, ot[...]).astype(BF16)
+
+    def send_heads(i):
         out = pl.ds(i * 64, 64)
-        made = [
-            push(hs.at[i, rows(at_t(k) * 64, 64), :], hm.at[t, out, :], dev_t(k)) for k in to_t
-        ]
+        for k in to_t:
+            heads_in.push(hs.at[i, rows(at_t(k) * 64, 64), :], hm.at[t, out, :], dev_t(k))
         hm[pl.ds(t, 1), out, :] = hs[i, rows(t * 64, 64), :][None]
-        return made
 
     row_i, lane_i = iota((256, 256), 0), iota((256, 256), 1)
 
@@ -299,37 +302,89 @@
             + (row_i & 3)
         ).astype(BF16)
 
+    def y_to_z():
+        return ones_where(
+            lane_i == ((row_i >> 3) & (ny - 1)) * 64 + (row_i >> 5) * 8 + (row_i & 7)
+        ).astype(BF16)
+
+    def z_to_g():
+        return ones_where(
+            lane_i
+            == ((row_i >> 2) & (NZ - 1)) * 32
+            + ((row_i >> 5) & (ny - 1)) * 8
+            + (row_i >> 7) * 4
+            + (row_i & 3)
+        ).astype(BF16)
+
+    hw = width // 2
+
     def send_y(buf, dst):
-        made = [push(buf.at[rows(at_y(k) * 64, 64), :], dst.at[y], dev_y(k)) for k in (1, 3, 2)]
+        group = push_all(
+            dst.at[pl.ds(0, ny - 1)],
+            [(buf.at[rows(at_y(k) * 64, 64), :], dst.at[y], dev_y(k)) for k in (1, 3, 2)],
+        )
         dst[pl.ds(y, 1)] = buf[rows(y * 64, 64), :][None]
-        return made
+        return group
 
     def send_z(buf, dst):
-        made = [
-            push(buf.at[rows(at_z(k) * 32, 32), :], dst.at[z], dev_z(k))
-            for k in (4, 3, 5, 2, 6, 1, 7)
-        ]
+        group = push_all(
+            dst.at[pl.ds(0, NZ - 1)],
+            [
+                (buf.at[rows(at_z(k) * 32, 32), :], dst.at[z], dev_z(k))
+                for k in (4, 3, 5, 2, 6, 1, 7)
+            ],
+        )
         dst[pl.ds(z, 1)] = buf[rows(z * 32, 32), :][None]
-        return made
+        return group
 
     def send_g(buf, dst):
-        made = [push(buf.at[rows((1 - g) * 128, 128), :], dst.at[g], dev_g)]
+        group = push_all(
+            dst.at[0], [(buf.at[rows((1 - g) * 128, 128), :], dst.at[g], dev_g)]
+        )
         dst[pl.ds(g, 1)] = buf[rows(g * 128, 128), :][None]
-        return made
-
-    def moved(order, src, dst):
-        for f in range(width // 256):
-            cols = slice(f * 256, (f + 1) * 256)
-            dst[:, cols] = mm(order, src(cols)).astype(BF16)
+        return group
+
+    class Exchange:
+        def __init__(self, buf, from_y, from_z, from_g):
+            self.buf, self.from_y, self.from_z, self.from_g = buf, from_y, from_z, from_g
+            self.group = [None, None]
+
+        def begin(self, order, src):
+            for j in range(2):
+                if j:
+                    order = mm(z_to_y(), order).astype(BF16)
+                self.buf[j] = mm(order, src[:, j * hw : (j + 1) * hw]).astype(BF16)
+                send, to = ((send_z, self.from_z), (send_y, self.from_y))[j]
+                self.group[j] = send(self.buf.at[j], to.at[j])
+
+        def next(self, j, came, order, send, to):
+            self.group[j].arrived()
+            self.group[j].sent()
+            self.buf[j] = mm(order(), came[j].reshape(256, hw)).astype(BF16)
+            self.group[j] = send(self.buf.at[j], to.at[j])
+
+        def second(self, j):
+            if j == 0:
+                self.next(0, self.from_z, z_to_y, send_y, self.from_y)
+            else:
+                self.next(1, self.from_y, y_to_z, send_z, self.from_z)
+
+        def third(self, j):
+            if j == 0:
+                self.next(0, self.from_y, y_to_g, send_g, self.from_g)
+            else:
+                self.next(1, self.from_z, z_to_g, send_g, self.from_g)
+
+        def end(self, order, dst):
+            for j in range(2):
+                self.group[j].arrived()
+                dst[:, j * hw : (j + 1) * hw] = mm(
+                    order, self.from_g[j].reshape(256, hw)
+                ).astype(BF16)
 
     forward_norm(0)
-    arrived(slots_y)
-    slots_z = [push(bty, btz.at[z], dev_z(k)) for k in range(1, NZ)]
-    btz[pl.ds(z, 1)] = bty[...][None]
     forward_qkv(0)
-    arrived(slots_z)
-    slots_g = [push(btz, btg.at[g], dev_g)]
-    btg[pl.ds(g, 1)] = btz[...][None]
+    forward_attend(0)
 
     pair = iota((256, 128), 0)
     block_lane = iota((256, 128), 1)
@@ -346,7 +401,32 @@
     to_row = jnp.sum(jnp.where(row_i == lane_i, to_at, 0.0), axis=0, keepdims=True).astype(I32)
     placing[1] = ones_where(row_i == to_row).astype(BF16)
 
-    arrived(slots_g)
+    pl.semaphore_wait(barrier, len(partners))
+
+    slots_y = push_all(
+        bty.at[pl.ds(0, ny - 1)], [(bts, bty.at[y], dev_y(k)) for k in range(1, ny)]
+    )
+    weight_part = wf.at[pl.ds(0, nt - 1), pl.ds(0, hrows), :]
+    weight_t = push_all(
+        weight_part,
+        [(ow_hbm.at[own_half, :], wf.at[t, own_half, :], dev_t(k)) for k in to_t],
+    )
+    heads_in = Group(hm.at[pl.ds(0, nt - 1)])
+    send_heads(0)
+    bty[pl.ds(y, 1)] = bts[...][None]
+
+    forward_norm(1)
+    slots_y.arrived()
+    slots_z = push_all(
+        btz.at[pl.ds(0, NZ - 1)], [(bty, btz.at[z], dev_z(k)) for k in range(1, NZ)]
+    )
+    btz[pl.ds(z, 1)] = bty[...][None]
+    forward_qkv(1)
+    slots_z.arrived()
+    slots_g = push_all(btg.at[0], [(btz, btg.at[g], dev_g)])
+    btg[pl.ds(g, 1)] = btz[...][None]
+    load_c.wait()
+    slots_g.arrived()
     lanes3 = (ny * NZ, 8, 128)
     sub3 = iota(lanes3, 1)
     both = jnp.where(sub3 < 4, btg[0].reshape(lanes3), btg[1].reshape(lanes3))
@@ -359,41 +439,40 @@
     sub1 = iota((ny * NZ, 8, 1), 1)
     slot_row = jnp.where((sub1 & 2) == 2, slot_1, slot_0) * 2.0 + (sub1 & 1).astype(F32)
     slot_row = slot_row.reshape(256, 1)
-    pick = ones_where(lane_i.astype(F32) == slot_row).astype(BF16)
-    load_c.wait()
-    moved(pick, lambda c: cot_ref[:, c], cs)
-    cot_z = send_z(cs, czr)
-
-    heads_in = forward_attend(0)
+    cot = Exchange(cs, cyr, czr, cgr)
+    cot.begin(ones_where(lane_i.astype(F32) == slot_row).astype(BF16), cot_ref)
     slot_lane = jnp.sum(jnp.where(row_i == lane_i, slot_row, 0.0), axis=0, keepdims=True)
     back_at = ones_where(row_i.astype(F32) == slot_lane).astype(BF16)
     returning[...] = mm(back_at, g_to_z()).astype(BF16)
 
-    forward_norm(1)
-    forward_qkv(1)
-    heads_in += forward_attend(1)
+    forward_attend(1)
+    send_heads(1)
     forward_norm(2)
     forward_qkv(2)
-    heads_in += forward_attend(2)
-    arrived(cot_z)
-    sent(cot_z)
-    moved(z_to_y(), lambda c: czr[:, :, c].reshape(256, 256), cs)
-    cot_y = send_y(cs, cyr)
-    arrived(weight_t)
-    weight_g = []
-    for k in range(1, nt):
-        piece = wf.at[at_t(nt - k), own_half, :]
-        weight_g.append(push(piece, piece, dev_g))
+    cot.second(1)
+    forward_attend(2)
+    send_heads(2)
     forward_norm(3)
     forward_qkv(3)
-    heads_in += forward_attend(3)
-    arrived(cot_y)
-    sent(cot_y)
-    moved(y_to_g(), lambda c: cyr[:, :, c].reshape(256, 256), cs)
-    cot_g = send_g(cs, cgr)
+    cot.second(0)
+    forward_attend(3)
+    send_heads(3)
+    weight_t.arrived()
+    weight_g = push_all(
+        weight_part,
+        [
+            (wf.at[at_t(nt - k), own_half, :], wf.at[at_t(nt - k), own_half, :], dev_g)
+            for k in to_t
+        ],
+    )
     load_o.wait()
-    arrived(heads_in)
-    arrived(weight_g)
+    cot.third(0)
+    heads_in.arrived()
+    wide = hcols - 128
+    for q in range(nt):
+        hmt[q] = mm_t(eye[:wide, :wide], hm[q, :, 128:]).astype(BF16)
+    cot.third(1)
+    weight_g.arrived()
 
     def project_out(c, _):
         cols = pl.ds(pl.multiple_of(c * 256, 256), 256)
@@ -404,8 +483,7 @@
         return 0
 
     lax.fori_loop(0, width // 256, project_out, 0)
-    arrived(cot_g)
-    moved(placing[0], lambda c: cgr[:, :, c].reshape(256, 256), inc)
+    cot.end(placing[0], inc)
 
     def merge_rows(c, _):
         at = pl.ds(pl.multiple_of(c * 32, 32), 32)
@@ -427,27 +505,26 @@
         q = at_t(k)
         ghs[pl.ds(q, 1)] = mm_t(wf[pl.ds(q, 1)].reshape(hcols, width), gown[...]).astype(BF16)[None]
     grads_in = [
-        [
-            push(
-                ghs.at[at_t(k), pl.ds(j * prows, prows), :],
-                ghr.at[t, pl.ds(j * prows, prows), :],
-                dev_t(k),
-            )
-            for k in to_t
-        ]
+        push_all(
+            ghr.at[pl.ds(0, nt - 1), pl.ds(0, prows), :],
+            [
+                (
+                    ghs.at[at_t(k), pl.ds(j * prows, prows), :],
+                    ghr.at[t, pl.ds(j * prows, prows), :],
+                    dev_t(k),
+                )
+                for k in to_t
+            ],
+        )
         for j in range(pairs)
     ]
     ghr[pl.ds(t, 1)] = ghs[pl.ds(t, 1)]
 
-    moved(placing[1], lambda c: merged[:, c], ms)
-    row_z = send_z(ms, mzr)
+    row = Exchange(ms, myr, mzr, mgr)
+    row.begin(placing[1], merged)
 
     for f in range(width // 256):
         gownt[f * 256 : (f + 1) * 256, :] = mm_t(eye, gown[:, f * 256 : (f + 1) * 256]).astype(BF16)
-    wide = hcols - 128
-    for q in range(nt):
-        hmt[q] = mm_t(eye[:wide, :wide], hm[q, :, 128:]).astype(BF16)
-
     def terms_b(side):
         def one(c, _):
             at = pl.ds(pl.multiple_of(side * half + c * (half // 2), 64), half // 2)
@@ -467,14 +544,12 @@
         oa[pl.ds(side, 1), pl.ds(q, 1)] = value.astype(BF16)[None, None]
 
     terms_b(1 - g)
-    b_g = [push(ob.at[1 - g], obg, dev_g)]
-    a_g = []
+    b = push_all(obg, [(ob.at[1 - g], obg, dev_g)])
+    a = []
     for k in to_t + (0,):
         terms_a(1 - g, k)
-        a_g.append([push(oa.at[1 - g, at_t(k)], oag.at[at_t(k)], dev_g)])
+        a.append(push_all(oag.at[0], [(oa.at[1 - g, at_t(k)], oag.at[at_t(k)], dev_g)]))
     terms_b(g)
-    for k in to_t + (0,):
-        terms_a(g, k)
 
     def spread(j):
         def one(i, _):
@@ -545,142 +620,155 @@
 
     def weight_start(h):
         weight_terms(h, 1 - g)
-        made = [push(dws.at[h, their_rows, :], dgr.at[h], dev_g)]
+        group = push_all(dgr.at[h], [(dws.at[h, their_rows, :], dgr.at[h], dev_g)])
         weight_terms(h, g)
-        return made
+        return group
 
     def weight_y(h, group):
-        arrived(group)
+        group.arrived()
         dgr[h] = add(dws[h, own_rows, :], dgr[h]).astype(BF16)
-        return [push(dgr.at[h, rows_y(k), :], dyr.at[h, j], dev_y(k)) for k, j in order_y]
+        return push_all(
+            dyr.at[h], [(dgr.at[h, rows_y(k), :], dyr.at[h, j], dev_y(k)) for k, j in order_y]
+        )
 
     def weight_z(h, group):
-        arrived(group)
+        group.arrived()
         total = dgr[h, rows_y(0), :].astype(F32)
         for k in range(1, ny):
             total += dyr[h, k - 1].astype(F32)
         dz[h] = mm(to_shards(), total.astype(BF16)).astype(BF16)
-        return [
-            push(dz.at[h, rows(at_z(k) * 32, 32), :], dzr.at[h, j], dev_z(k)) for k, j in order_z
-        ]
+        return push_all(
+            dzr.at[h],
+            [(dz.at[h, rows(at_z(k) * 32, 32), :], dzr.at[h, j], dev_z(k)) for k, j in order_z],
+        )
 
     def weight_end(h, group):
-        arrived(group)
+        group.arrived()
         total = dz[h, rows(z * 32, 32), :].astype(F32)
         for k in range(1, NZ):
             total += dzr[h, k - 1].astype(F32)
-        gq_ref[h] = total
+        gq_ref[:, h * 3 * HEAD_V : (h + 1) * 3 * HEAD_V] = total[:zrows]
 
     def b_y(group):
-        arrived(group)
+        group.arrived()
         obg[...] = add(ob[pl.ds(g, 1)].reshape(half, nt * 128), obg[...]).astype(BF16)
-        return [push(obg.at[rows_y(k), :], obyr.at[j], dev_y(k)) for k, j in order_y]
+        return push_all(obyr, [(obg.at[rows_y(k), :], obyr.at[j], dev_y(k)) for k, j in order_y])
 
     def b_x(group):
-        arrived(group)
+        group.arrived()
         total = obg[rows_y(0), :].astype(F32)
         for k in range(1, ny):
             total += obyr[k - 1].astype(F32)
         for q in range(nt):
             obx[q] = total[:, q * 128 : (q + 1) * 128].astype(BF16)
-        return [push(obx.at[at_t(k)], obxr.at[k - 1], dev_t(k)) for k in to_t]
+        return push_all(obxr, [(obx.at[at_t(k)], obxr.at[k - 1], dev_t(k)) for k in to_t])
 
     def b_z(group):
-        arrived(group)
+        group.arrived()
         total = obx[pl.ds(t, 1)].reshape(yrows, 128).astype(F32)
         for k in range(1, nt):
             total += obxr[k - 1].astype(F32)
         obz[...] = mm(to_shards(), total.astype(BF16)).astype(BF16)
-        return [push(obz.at[rows(at_z(k) * 32, 32), :], obzr.at[j], dev_z(k)) for k, j in order_z]
+        return push_all(
+            obzr, [(obz.at[rows(at_z(k) * 32, 32), :], obzr.at[j], dev_z(k)) for k, j in order_z]
+        )
 
     def b_end(group):
-        arrived(group)
+        group.arrived()
         total = obz[rows(z * 32, 32), :].astype(F32)
         for k in range(1, NZ):
             total += obzr[k - 1].astype(F32)
-        go_ref[:, :128] = total
+        go_ref[:, :128] = total[:zrows]
 
     def a_x(groups):
-        made = []
+        out = Group(oax)
         for k, group in zip(to_t + (0,), groups):
-            arrived(group)
+            group.arrived()
             q = at_t(k)
             mine = oa[pl.ds(g, 1), pl.ds(q, 1)].reshape(wide, half)
             oag[pl.ds(q, 1)] = add(mine, oag[pl.ds(q, 1)].reshape(wide, half)).astype(BF16)[None]
             if k:
-                made.append(push(oag.at[q], oax.at[k - 1], dev_t(k)))
-        return made
+                out.push(oag.at[q], oax.at[k - 1], dev_t(k))
+        return out
 
     def a_y(group):
-        arrived(group)
+        group.arrived()
         for f in range(half // 128):
             cols = slice(f * 128, (f + 1) * 128)
             total = oag[pl.ds(t, 1), :, cols].reshape(wide, 128).astype(F32)
             for k in range(1, nt):
                 total += oax[k - 1, :, cols].astype(F32)
             oay[cols, :] = mm_t(eye[:128, :128], total.astype(BF16)).astype(BF16)
-        return [push(oay.at[rows_y(k), :], oayr.at[j], dev_y(k)) for k, j in order_y]
+        return push_all(oayr, [(oay.at[rows_y(k), :], oayr.at[j], dev_y(k)) for k, j in order_y])
 
     def a_z(group):
-        arrived(group)
+        group.arrived()
         total = oay[rows_y(0), :].astype(F32)
         for k in range(1, ny):
             total += oayr[k - 1].astype(F32)
         oaz[...] = mm(to_shards(), total.astype(BF16)).astype(BF16)
-        return [push(oaz.at[rows(at_z(k) * 32, 32), :], oazr.at[j], dev_z(k)) for k, j in order_z]
+        return push_all(
+            oazr, [(oaz.at[rows(at_z(k) * 32, 32), :], oazr.at[j], dev_z(k)) for k, j in order_z]
+        )
 
     def a_end(group):
-        arrived(group)
+        group.arrived()
         total = oaz[rows(z * 32, 32), :].astype(F32)
         for k in range(1, NZ):
             total += oazr[k - 1].astype(F32)
-        go_ref[:, 128:] = total
-
-    arrived(grads_in[0])
+        go_ref[:, 128:] = total[:zrows]
+
+    b = b_y(b)
+    for k in to_t + (0,):
+        terms_a(g, k)
+    grads_in[0].arrived()
     spread(0)
     back_head(0)
-    b = b_y(b_g)
-    a = a_x(a_g)
+    a = a_x(a)
     w0 = weight_start(0)
+    row.second(1)
     back_head(1)
     w0 = weight_y(0, w0)
+    row.second(0)
     w1 = weight_start(1)
-    arrived(grads_in[1])
+    grads_in[1].arrived()
     spread(1)
+    b = b_x(b)
     back_head(2)
     w1 = weight_y(1, w1)
     w2 = weight_start(2)
-    arrived(row_z)
-    sent(row_z)
-    moved(z_to_y(), lambda c: mzr[:, :, c].reshape(256, 256), ms)
-    row_y = send_y(ms, myr)
     w0 = weight_z(0, w0)
-    b = b_x(b)
+    b = b_z(b)
     back_head(3)
     w2 = weight_y(2, w2)
     w3 = weight_start(3)
     w1 = weight_z(1, w1)
+    row.third(0)
     w3 = weight_y(3, w3)
-    b = b_z(b)
     a = a_y(a)
+    row.third(1)
     w2 = weight_z(2, w2)
-    arrived(row_y)
-    sent(row_y)
-    moved(y_to_g(), lambda c: myr[:, :, c].reshape(256, 256), ms)
-    row_g = send_g(ms, mgr)
     weight_end(0, w0)
+    b_end(b)
     w3 = weight_z(3, w3)
+    row.end(returning[...], image)
+    store_i = pltpu.make_async_copy(image, image_hbm, lsem.at[images + 3])
+    store_i.start()
     a = a_z(a)
     weight_end(1, w1)
-    b_end(b)
-    arrived(row_g)
-    moved(returning[...], lambda c: mgr[:, :, c].reshape(256, 256), image_ref)
     weight_end(2, w2)
     weight_end(3, w3)
     a_end(a)
-    for c in copies.values():
-        c.wait_send()
+    store_i.wait()
+    for group in list(open_sends.values()):
+        group.sent()
     assert used[0] == n_sems
+
+
+def hand_over(a, b, c, a_out, b_out, c_out):
+    a_out[...] = a[...]
+    b_out[...] = b[...]
+    c_out[...] = c[...]
 
 
 def shards(
@@ -693,17 +781,8 @@
     cols = 3 * HEAD_V
     half, yrows = width // 2, width // 2 // ny
     wide = hcols - 128
-    to_all = NZ - 1 + ny - 1 + 1
-    n_sems = (
-        to_all
-        + 2 * (nt - 1)
-        + images * (nt - 1)
-        + 2 * to_all
-        + 2 * (nt - 1)
-        + to_all + nt - 1
-        + to_all + 2 * nt - 2
-        + heads * to_all
-    )
+    zrows = yrows // NZ
+    n_sems = 3 + 2 + 1 + 6 + 6 + 2 + 4 + (nt + 3) + 3 * heads
     v = pltpu.VMEM
     scratch = [
         v((row_count, width), BF16),
@@ -724,14 +803,15 @@
         v((2, NZ, ny, 8, 128), I32),
         v((2, 256, 256), BF16),
         v((256, 256), BF16),
+        v((2, 256, half), BF16),
+        v((2, ny, 64, half), BF16),
+        v((2, NZ, 32, half), BF16),
+        v((2, 2, 128, half), BF16),
+        v((2, 256, half), BF16),
+        v((2, ny, 64, half), BF16),
+        v((2, NZ, 32, half), BF16),
+        v((2, 2, 128, half), BF16),
         v((256, width), BF16),
-        v((ny, 64, width), BF16),
-        v((NZ, 32, width), BF16),
-        v((2, 128, width), BF16),
-        v((256, width), BF16),
-        v((ny, 64, width), BF16),
-        v((NZ, 32, width), BF16),
-        v((2, 128, width), BF16),
         v((256, width), BF16),
         v((256, width), BF16),
         v((256, width), BF16),
@@ -759,7 +839,7 @@
         v((heads, ny - 1, yrows, cols), BF16),
         v((heads, NZ * 32, cols), BF16),
         v((heads, NZ - 1, 32, cols), BF16),
-        pltpu.SemaphoreType.DMA((images + 3,)),
+        pltpu.SemaphoreType.DMA((images + 4,)),
         pltpu.SemaphoreType.DMA((n_sems,)),
         pltpu.SemaphoreType.DMA((n_sems,)),
     ]
@@ -769,11 +849,11 @@
         functools.partial(kernel, ny, nt, n_sems),
         out_shape=(
             jax.ShapeDtypeStruct((256, width), BF16),
-            jax.ShapeDtypeStruct((heads, 32, cols), F32),
-            jax.ShapeDtypeStruct((32, hcols), F32),
+            jax.ShapeDtypeStruct((zrows, heads * cols), F32),
+            jax.ShapeDtypeStruct((zrows, hcols), F32),
         ),
         in_specs=[pl.BlockSpec(memory_space=pltpu.SMEM)] + [in_vmem] * 3 + [in_hbm] * 4,
-        out_specs=(in_vmem,) * 3,
+        out_specs=(in_hbm, in_vmem, in_vmem),
         scratch_shapes=scratch,
         compiler_params=pltpu.CompilerParams(
             collective_id=0, has_side_effects=True, vmem_limit_bytes=62 << 20
@@ -789,10 +869,14 @@
         out_weight,
         cotangent,
     )
-    zrows = yrows // NZ
-    grad_qkv = jnp.moveaxis(gq[:, :zrows], 0, 1).reshape(zrows, heads * cols)
-    grad_out = go[:zrows].T
-    return image_rows, grad_qkv, grad_out
+    image_rows, grad_qkv, grad_out = pl.pallas_call(
+        hand_over,
+        out_shape=tuple(jax.ShapeDtypeStruct(a.shape, a.dtype) for a in (image_rows, gq, go)),
+        in_specs=[in_vmem] * 3,
+        out_specs=(in_vmem,) * 3,
+        name="hand_over",
+    )(image_rows, gq, go)
+    return image_rows, grad_qkv, grad_out.T
 
 
 def solution(mesh):

time: 113 us -> 103 us (0.912)
  local copies, waits for them, and re-layouts: 5.04 us -> 0 us
  Pallas kernels: 107 us -> 102 us
    pallas_call x1, Pallas kernels: 107 us -> 99.9 us  [shards(): pl.pallas_call(functools.partial(kernel, ny, nt, n_sems), out_shape=(jax....]
    transpose x3 -> x0, local copies, waits for them, and re-layouts: 2.32 us -> none  [the longest x1 1.39 us: shards(): grad_out = go[:zrows].T]
    pallas_call x0 -> x1, Pallas kernels: none -> 2.04 us  [shards(): pl.pallas_call(hand_over, out_shape=tuple((jax.ShapeDtypeStruct(a.shape,...]
    unnamed x1 -> x0, local copies, waits for them, and re-layouts: 1.96 us -> none
where the time goes in v2:
time: 103 us
  Pallas kernels  102 us (99%)
    pallas_call x1, Pallas kernels, shards(): pl.pallas_call(functools.partial(kernel, ny, nt, n_sems), out_shape=(jax....  99.9 us

profile of v2, /device:TPU:1, one launch (start us, length us, event | category | flops | bytes accessed | tf_op | source)
XLA Modules:
  0.0 102.6 jit_solution(16676403587299217796)
XLA Ops:
  0.6 99.9 %block.1 = (bf16[256,1280]{1,0:T(8,128)(2,1)}, f32[20,960]{1,0:T(8,128)}, f32[20,320]{1,0:T(8,128)}) custom-call(s32[4]{0:T(128)} %counts.1, f32[1280]{0:T(1024)} %ga_ref.1, f32[1280]{0:T(1024)} %gm_ref.1, s32[1,128]{1,0:T(1,128)} %bitcast.4, bf16[1024,1280]{1,0:T(8,128)(2,1)} %x_hbm.1, bf16[960,1280]{1,0:T(8,128)(2,1)} %bitcast.3, ...), custom_call_target="tpu_custom_call" | custom-call | tf_op jit(solution)/shard_map/block/pallas_call | solution.py:848
  100.5 2.0 %hand_over.1 = (bf16[256,1280]{1,0:T(8,128)(2,1)}, f32[20,960]{1,0:T(8,128)}, f32[20,320]{1,0:T(8,128)}) custom-call(bf16[256,1280]{1,0:T(8,128)(2,1)} %get-tuple-element.9.a, f32[20,960]{1,0:T(8,128)} %get-tuple-element.10.b, f32[20,320]{1,0:T(8,128)} %get-tuple-element.11.c), custom_call_target="tpu_custom_call" | custom-call | tf_op jit(solution)/shard_map/hand_over/pallas_call | solution.py:872

commit v3 on v2

--- a/solution.py
+++ b/solution.py
@@ -228,7 +228,7 @@
             nrm[at, :] = (center * scale * gain_a).astype(BF16)
             return 0
 
-        lax.fori_loop(0, 8, norm_rows, 0)
+        lax.fori_loop(0, 8, norm_rows, 0, unroll=2)
         own = ones_where(iota((64, 256), 1) == 4 * iota((64, 256), 0) + t).astype(BF16)
         res[base // 4 : base // 4 + 64, :] = mm(own, x_ref[base : base + 256, :])
         for f in range(width // 256):
@@ -497,27 +497,26 @@
         gown[at, :] = (scale * (grad - mean_grad - hat * mean_hat)).astype(BF16)
         return 0
 
-    lax.fori_loop(0, 8, merge_rows, 0)
+    lax.fori_loop(0, 8, merge_rows, 0, unroll=2)
 
     pairs = 2
     prows = hcols // pairs
-    for k in to_t + (0,):
+    grads_in = [Group(ghr.at[pl.ds(0, nt - 1), pl.ds(0, prows), :]) for _ in range(pairs)]
+
+    def grads_for(k):
         q = at_t(k)
         ghs[pl.ds(q, 1)] = mm_t(wf[pl.ds(q, 1)].reshape(hcols, width), gown[...]).astype(BF16)[None]
-    grads_in = [
-        push_all(
-            ghr.at[pl.ds(0, nt - 1), pl.ds(0, prows), :],
-            [
-                (
-                    ghs.at[at_t(k), pl.ds(j * prows, prows), :],
-                    ghr.at[t, pl.ds(j * prows, prows), :],
-                    dev_t(k),
-                )
-                for k in to_t
-            ],
-        )
-        for j in range(pairs)
-    ]
+
+    def send_grads(j, k):
+        part = pl.ds(j * prows, prows)
+        grads_in[j].push(ghs.at[at_t(k), part, :], ghr.at[t, part, :], dev_t(k))
+
+    for k in to_t:
+        grads_for(k)
+        send_grads(0, k)
+    for k in to_t:
+        send_grads(1, k)
+    grads_for(0)
     ghr[pl.ds(t, 1)] = ghs[pl.ds(t, 1)]
 
     row = Exchange(ms, myr, mzr, mgr)
@@ -591,7 +590,7 @@
             qkvt[at_v : at_v + HEAD_V, cols] = grad_v
             return 0
 
-        lax.fori_loop(0, images, back_image, 0)
+        lax.fori_loop(0, images, back_image, 0, unroll=4)
 
     def weight_terms(h, side):
         def one(c, _):
@@ -739,26 +738,26 @@
     w2 = weight_start(2)
     w0 = weight_z(0, w0)
     b = b_z(b)
+    a = a_y(a)
     back_head(3)
     w2 = weight_y(2, w2)
+    w1 = weight_z(1, w1)
     w3 = weight_start(3)
-    w1 = weight_z(1, w1)
     row.third(0)
+    a = a_z(a)
     w3 = weight_y(3, w3)
-    a = a_y(a)
     row.third(1)
     w2 = weight_z(2, w2)
     weight_end(0, w0)
     b_end(b)
+    weight_end(1, w1)
     w3 = weight_z(3, w3)
     row.end(returning[...], image)
     store_i = pltpu.make_async_copy(image, image_hbm, lsem.at[images + 3])
     store_i.start()
-    a = a_z(a)
-    weight_end(1, w1)
+    a_end(a)
     weight_end(2, w2)
     weight_end(3, w3)
-    a_end(a)
     store_i.wait()
     for group in list(open_sends.values()):
         group.sent()

time: 103 us -> 97.4 us (0.946)
  Pallas kernels: 102 us -> 96.6 us
    pallas_call x1, Pallas kernels: 99.9 us -> 94.6 us  [shards(): pl.pallas_call(functools.partial(kernel, ny, nt, n_sems), out_shape=(jax....]
where the time goes in v3:
time: 97.4 us; the launch traced here: 97.2 us
  Pallas kernels  96.6 us (99%)
    pallas_call x1, Pallas kernels, shards(): pl.pallas_call(functools.partial(kernel, ny, nt, n_sems), out_shape=(jax....  94.6 us
    pallas_call x1, Pallas kernels, shards(): pl.pallas_call(hand_over, out_shape=tuple((jax.ShapeDtypeStruct(a.shape,...  2.04 us

profile of v3, /device:TPU:1, one launch (start us, length us, event | category | flops | bytes accessed | tf_op | source)
XLA Modules:
  0.0 97.2 jit_solution(1965654475323999603)
XLA Ops:
  0.6 94.6 %block.1 = (bf16[256,1280]{1,0:T(8,128)(2,1)}, f32[20,960]{1,0:T(8,128)}, f32[20,320]{1,0:T(8,128)}) custom-call(s32[4]{0:T(128)} %counts.1, f32[1280]{0:T(1024)} %ga_ref.1, f32[1280]{0:T(1024)} %gm_ref.1, s32[1,128]{1,0:T(1,128)} %bitcast.4, bf16[1024,1280]{1,0:T(8,128)(2,1)} %x_hbm.1, bf16[960,1280]{1,0:T(8,128)(2,1)} %bitcast.3, ...), custom_call_target="tpu_custom_call" | custom-call | tf_op jit(solution)/shard_map/block/pallas_call | solution.py:847
  95.2 2.0 %hand_over.1 = (bf16[256,1280]{1,0:T(8,128)(2,1)}, f32[20,960]{1,0:T(8,128)}, f32[20,320]{1,0:T(8,128)}) custom-call(bf16[256,1280]{1,0:T(8,128)(2,1)} %get-tuple-element.9.a, f32[20,960]{1,0:T(8,128)} %get-tuple-element.10.b, f32[20,320]{1,0:T(8,128)} %get-tuple-element.11.c), custom_call_target="tpu_custom_call" | custom-call | tf_op jit(solution)/shard_map/hand_over/pallas_call | solution.py:871

commit v4 on v3

--- a/solution.py
+++ b/solution.py
@@ -228,7 +228,7 @@
             nrm[at, :] = (center * scale * gain_a).astype(BF16)
             return 0
 
-        lax.fori_loop(0, 8, norm_rows, 0, unroll=2)
+        lax.fori_loop(0, 8, norm_rows, 0, unroll=4)
         own = ones_where(iota((64, 256), 1) == 4 * iota((64, 256), 0) + t).astype(BF16)
         res[base // 4 : base // 4 + 64, :] = mm(own, x_ref[base : base + 256, :])
         for f in range(width // 256):
@@ -246,7 +246,7 @@
             qkvt[at, base : base + 256] = mm_t(wt[at, :], nrm[...]).astype(BF16)
             return 0
 
-        lax.fori_loop(0, 3 * hcols // 240, project, 0)
+        lax.fori_loop(0, 3 * hcols // 240, project, 0, unroll=2)
 
     def forward_attend(i):
         base = i * 256
@@ -497,7 +497,7 @@
         gown[at, :] = (scale * (grad - mean_grad - hat * mean_hat)).astype(BF16)
         return 0
 
-    lax.fori_loop(0, 8, merge_rows, 0, unroll=2)
+    lax.fori_loop(0, 8, merge_rows, 0, unroll=4)
 
     pairs = 2
     prows = hcols // pairs
@@ -560,7 +560,7 @@
             ght[j * prows : (j + 1) * prows, cols] = total.astype(BF16)
             return 0
 
-        lax.fori_loop(0, images, one, 0)
+        lax.fori_loop(0, images, one, 0, unroll=2)
 
     def back_head(h):
         row = h * 3 * HEAD_V
@@ -600,7 +600,7 @@
             ).astype(BF16)
             return 0
 
-        lax.fori_loop(0, 2, one, 0)
+        lax.fori_loop(0, 2, one, 0, unroll=2)
 
     def to_shards():
         r, c = iota((NZ * 32, yrows), 0), iota((NZ * 32, yrows), 1)

time: 97.4 us -> 94.8 us (0.973)
  Pallas kernels: 96.6 us -> 94.1 us
    pallas_call x1, Pallas kernels: 94.6 us -> 92 us  [shards(): pl.pallas_call(functools.partial(kernel, ny, nt, n_sems), out_shape=(jax....]
where the time goes in v4:
time: 94.8 us; the launch traced here: 94.7 us
  Pallas kernels  94.1 us (99%)
    pallas_call x1, Pallas kernels, shards(): pl.pallas_call(functools.partial(kernel, ny, nt, n_sems), out_shape=(jax....  92 us
    pallas_call x1, Pallas kernels, shards(): pl.pallas_call(hand_over, out_shape=tuple((jax.ShapeDtypeStruct(a.shape,...  2.04 us

profile of v4, /device:TPU:1, one launch (start us, length us, event | category | flops | bytes accessed | tf_op | source)
XLA Modules:
  0.0 94.7 jit_solution(6084893904161260685)
XLA Ops:
  0.6 92.0 %block.1 = (bf16[256,1280]{1,0:T(8,128)(2,1)}, f32[20,960]{1,0:T(8,128)}, f32[20,320]{1,0:T(8,128)}) custom-call(s32[4]{0:T(128)} %counts.1, f32[1280]{0:T(1024)} %ga_ref.1, f32[1280]{0:T(1024)} %gm_ref.1, s32[1,128]{1,0:T(1,128)} %bitcast.4, bf16[1024,1280]{1,0:T(8,128)(2,1)} %x_hbm.1, bf16[960,1280]{1,0:T(8,128)(2,1)} %bitcast.3, ...), custom_call_target="tpu_custom_call" | custom-call | tf_op jit(solution)/shard_map/block/pallas_call | solution.py:847
  92.7 2.0 %hand_over.1 = (bf16[256,1280]{1,0:T(8,128)(2,1)}, f32[20,960]{1,0:T(8,128)}, f32[20,320]{1,0:T(8,128)}) custom-call(bf16[256,1280]{1,0:T(8,128)(2,1)} %get-tuple-element.9.a, f32[20,960]{1,0:T(8,128)} %get-tuple-element.10.b, f32[20,320]{1,0:T(8,128)} %get-tuple-element.11.c), custom_call_target="tpu_custom_call" | custom-call | tf_op jit(solution)/shard_map/hand_over/pallas_call | solution.py:871
